TPU v7x, 256 devices: a whole 4x4x8 slice. The times are simulated.
256 devices in a mesh: seq: 16 (over y, x), head: 8 (over z), dp: 2 (over core).
Axes of the slice: x: 4, y: 4, z: 8, core: 2. Of those that a mesh axis runs over, the one named last changes fastest.
Arguments:
- query_heads: bfloat16 [2, 4096, 4096], P('dp', 'seq', 'head'), may hold values from -100 to 100
- key_heads: bfloat16 [2, 4096, 4096], P('dp', 'seq', 'head'), may hold values from -100 to 100
- value_heads: bfloat16 [2, 4096, 4096], P('dp', 'seq', 'head'), may hold values from -6 to 6
- query_gain: float32 [4096], P('head'), may hold values from 0.5 to 1.5
- key_gain: float32 [4096], P('head'), may hold values from 0.5 to 1.5
- key_squeeze: bfloat16 [32, 512, 128], P('head'), may hold values from -0.25 to 0.25
- value_squeeze: bfloat16 [32, 512, 128], P('head'), may hold values from -0.25 to 0.25
- grad_out: bfloat16 [2, 4096, 4096], P('dp', 'seq', 'head'), may hold values from -6 to 6
Outputs:
- grad_query: bfloat16 [2, 4096, 4096], P('dp', 'seq', 'head')
- grad_key: bfloat16 [2, 4096, 4096], P('dp', 'seq', 'head')
- grad_value: bfloat16 [2, 4096, 4096], P('dp', 'seq', 'head')
- grad_query_gain: float32 [4096], P('head')
- grad_key_gain: float32 [4096], P('head')
- grad_key_squeeze: float32 [32, 512, 128], P('head')
- grad_value_squeeze: float32 [32, 512, 128], P('head')
All inputs are finite; a program needn't handle non-finite values.
Results may differ from a plain program's by a relative error of at most 0.025.
Values may be sent and summed in bfloat16 or wider, within the bound.
A program may use at most 64 MiB of HBM per device.

v0:
```python
import jax
import jax.numpy as jnp
from jax import lax
from jax.sharding import PartitionSpec as P

HD = 128
KS = 4
HH = 4096


epsilon = 1e-06


def unfold_slots(source, head_count):
    batch_size, row_count, widths = source.shape
    return (
        source.reshape(batch_size, row_count // KS, KS, head_count, HD)
        .transpose(0, 1, 3, 2, 4)
        .reshape(batch_size, row_count // KS, head_count, KS * HD)
    )


def fold_slots(source):
    batch_size, slot_count, head_count, spans = source.shape
    return (
        source.reshape(batch_size, slot_count, head_count, KS, HD)
        .transpose(0, 1, 3, 2, 4)
        .reshape(batch_size, slot_count * KS, head_count * HD)
    )


def on_device(
    query_heads, key_heads, value_heads, query_gain, key_gain, key_squeeze, value_squeeze, grad_out
):
    batch_size, row_count, widths = query_heads.shape
    head_count = widths // HD
    slot_count = row_count // KS
    memory_rows = slot_count * lax.axis_size("seq")
    score_scale = HD ** (-0.5)
    own_limit = lax.axis_index("seq") * slot_count
    q_full = query_heads.astype(jnp.float32)
    k_full = key_heads.astype(jnp.float32)
    sum_q, sum_k = lax.psum((jnp.sum(q_full * q_full, -1), jnp.sum(k_full * k_full, -1)), "head")
    inv_q = lax.rsqrt(sum_q / HH + epsilon)[..., None]
    inv_k = lax.rsqrt(sum_k / HH + epsilon)[..., None]
    q_norm = (q_full * inv_q * query_gain).astype(jnp.bfloat16)
    k_norm = (k_full * inv_k * key_gain).astype(jnp.bfloat16)
    k_unf = unfold_slots(k_norm, head_count)
    v_unf = unfold_slots(value_heads, head_count)
    mem_k = (
        jnp.einsum("bmhc,hcd->bmhd", k_unf, key_squeeze, preferred_element_type=jnp.float32)
        .astype(jnp.bfloat16)
        .reshape(batch_size, slot_count, widths)
    )
    mem_v = (
        jnp.einsum("bmhc,hcd->bmhd", v_unf, value_squeeze, preferred_element_type=jnp.float32)
        .astype(jnp.bfloat16)
        .reshape(batch_size, slot_count, widths)
    )
    queries = q_norm.reshape(batch_size, row_count, head_count, HD)
    key_loc = k_norm.reshape(batch_size, row_count, head_count, HD)
    value_loc = value_heads.reshape(batch_size, row_count, head_count, HD)
    cotangent = grad_out.reshape(batch_size, row_count, head_count, HD)
    positions = jnp.arange(row_count)
    causal = positions[:, None] >= positions[None, :]
    scores_loc = jnp.where(
        causal,
        jnp.einsum("bthd,buhd->bhtu", queries, key_loc, preferred_element_type=jnp.float32)
        * score_scale,
        -jnp.inf,
    )
    grads_loc = jnp.einsum(
        "bthd,buhd->bhtu", cotangent, value_loc, preferred_element_type=jnp.float32
    )

    def memory_scores(piece_k, piece_v):
        piece_rows = piece_k.shape[1]
        key_rows = piece_k.reshape(batch_size, piece_rows, head_count, HD)
        value_rows = piece_v.reshape(batch_size, piece_rows, head_count, HD)
        allowed = jnp.arange(piece_rows) < own_limit
        scores = jnp.where(
            allowed,
            jnp.einsum("bthd,buhd->bhtu", queries, key_rows, preferred_element_type=jnp.float32)
            * score_scale,
            -jnp.inf,
        )
        gradients = jnp.einsum(
            "bthd,buhd->bhtu", cotangent, value_rows, preferred_element_type=jnp.float32
        )
        return (key_rows, scores, gradients)

    def memory_terms(key_rows, scores, gradients, log_mass, row_delta):
        piece_rows = key_rows.shape[1]
        attend = jnp.exp(scores - log_mass[..., None])
        d_scores = (attend * (gradients - row_delta[..., None])).astype(jnp.bfloat16)
        grad_q = score_scale * jnp.einsum(
            "bhtu,buhd->bthd", d_scores, key_rows, preferred_element_type=jnp.float32
        )
        grad_k = score_scale * jnp.einsum(
            "bhtu,bthd->buhd", d_scores, queries, preferred_element_type=jnp.float32
        )
        grad_v = jnp.einsum(
            "bhtu,bthd->buhd",
            attend.astype(jnp.bfloat16),
            cotangent,
            preferred_element_type=jnp.float32,
        )
        stacked = jnp.stack(
            (
                grad_k.reshape(batch_size, piece_rows, widths),
                grad_v.reshape(batch_size, piece_rows, widths),
            )
        )
        return (grad_q, stacked)

    peak_loc = jnp.max(scores_loc, -1)
    lifted_loc = jnp.exp(scores_loc - peak_loc[..., None])
    start_state = (peak_loc, jnp.sum(lifted_loc, -1), jnp.sum(lifted_loc * grads_loc, -1))
    pieces = (
        lax.all_gather(mem_k, "seq", axis=1, tiled=True),
        lax.all_gather(mem_v, "seq", axis=1, tiled=True),
    )

    def absorb_active(current):
        peak, summed, weighted = current
        unused, scores, gradients = memory_scores(pieces[0], pieces[1])
        new_peak = jnp.maximum(peak, jnp.max(scores, -1))
        factor = jnp.exp(peak - new_peak)
        lifted = jnp.exp(scores - new_peak[..., None])
        return (
            new_peak,
            summed * factor + jnp.sum(lifted, -1),
            weighted * factor + jnp.sum(lifted * gradients, -1),
        )

    peak, summed, weighted = lax.cond(
        jnp.int32(0) < own_limit, absorb_active, lambda current: current, start_state
    )
    log_mass = peak + jnp.log(summed)
    row_delta = weighted / summed
    empty = (
        jnp.zeros(queries.shape, jnp.float32),
        jnp.zeros((2, batch_size, memory_rows, widths), jnp.float32),
    )
    collect_pieces = (
        lax.all_gather(mem_k, "seq", axis=1, tiled=True),
        lax.all_gather(mem_v, "seq", axis=1, tiled=True),
    )

    def collect_active(current):
        key_rows, scores, gradients = memory_scores(collect_pieces[0], collect_pieces[1])
        grad_piece, term_piece = memory_terms(key_rows, scores, gradients, log_mass, row_delta)
        return (grad_piece, term_piece)

    grad_q_mem, term = lax.cond(
        jnp.int32(0) < own_limit, collect_active, lambda current: current, empty
    )
    attend_loc = jnp.exp(scores_loc - log_mass[..., None])
    d_loc = (attend_loc * (grads_loc - row_delta[..., None])).astype(jnp.bfloat16)
    grad_qn = (
        score_scale
        * jnp.einsum("bhtu,buhd->bthd", d_loc, key_loc, preferred_element_type=jnp.float32)
        + grad_q_mem
    ).reshape(batch_size, row_count, widths)
    grad_kn_local = score_scale * jnp.einsum(
        "bhtu,bthd->buhd", d_loc, queries, preferred_element_type=jnp.float32
    )
    grad_v_local = jnp.einsum(
        "bhtu,bthd->buhd",
        attend_loc.astype(jnp.bfloat16),
        cotangent,
        preferred_element_type=jnp.float32,
    )
    mine = lax.psum_scatter(term.astype(jnp.bfloat16), "seq", scatter_dimension=2, tiled=True)
    grad_mem_k = mine[0].reshape(batch_size, slot_count, head_count, HD)
    grad_mem_v = mine[1].reshape(batch_size, slot_count, head_count, HD)
    squeeze_k_part = jnp.einsum(
        "bmhc,bmhd->hcd", k_unf, grad_mem_k, preferred_element_type=jnp.float32
    )
    squeeze_v_part = jnp.einsum(
        "bmhc,bmhd->hcd", v_unf, grad_mem_v, preferred_element_type=jnp.float32
    )
    back_k = fold_slots(
        jnp.einsum("bmhd,hcd->bmhc", grad_mem_k, key_squeeze, preferred_element_type=jnp.float32)
    )
    back_v = fold_slots(
        jnp.einsum("bmhd,hcd->bmhc", grad_mem_v, value_squeeze, preferred_element_type=jnp.float32)
    )
    grad_kn = grad_kn_local.reshape(batch_size, row_count, widths) + back_k
    grad_value = (grad_v_local.reshape(batch_size, row_count, widths) + back_v).astype(jnp.bfloat16)
    dot_q, dot_k = lax.psum(
        (jnp.sum(query_gain * grad_qn * q_full, -1), jnp.sum(key_gain * grad_kn * k_full, -1)),
        "head",
    )
    grad_query = (
        inv_q * query_gain * grad_qn - q_full * inv_q**3 * dot_q[..., None] / HH
    ).astype(jnp.bfloat16)
    grad_key = (inv_k * key_gain * grad_kn - k_full * inv_k**3 * dot_k[..., None] / HH).astype(
        jnp.bfloat16
    )
    gain_q_part = jnp.sum(grad_qn * q_full * inv_q, (0, 1))
    gain_k_part = jnp.sum(grad_kn * k_full * inv_k, (0, 1))
    grad_query_gain, grad_key_gain, grad_key_squeeze, grad_value_squeeze = (
        lax.psum(gain_q_part.astype(jnp.bfloat16), ("seq", "dp")).astype(jnp.float32),
        lax.psum(gain_k_part.astype(jnp.bfloat16), ("seq", "dp")).astype(jnp.float32),
        lax.psum(squeeze_k_part.astype(jnp.bfloat16), ("seq", "dp")).astype(jnp.float32),
        lax.psum(squeeze_v_part.astype(jnp.bfloat16), ("seq", "dp")).astype(jnp.float32),
    )
    return (
        grad_query,
        grad_key,
        grad_value,
        grad_query_gain,
        grad_key_gain,
        grad_key_squeeze,
        grad_value_squeeze,
    )


def solution(mesh):
    placed = (
        P("dp", "seq", "head"),
        P("dp", "seq", "head"),
        P("dp", "seq", "head"),
        P("head"),
        P("head"),
        P("head", None, None),
        P("head", None, None),
        P("dp", "seq", "head"),
    )
    return jax.shard_map(
        on_device,
        mesh=mesh,
        in_specs=placed,
        out_specs=(
            P("dp", "seq", "head"),
            P("dp", "seq", "head"),
            P("dp", "seq", "head"),
            P("head"),
            P("head"),
            P("head", None, None),
            P("head", None, None),
        ),
        check_vma=False,
    )
```

profile of v0, /device:TPU:1, one launch (start us, length us, event | category | flops | bytes accessed | tf_op | source)
XLA Modules:
  0.0 398.5 jit_solution(1852459861606496026)
XLA Ops:
  7.3 1.2 fusion.36
  9.5 17.3 %all-reduce.2 = (f32[1,256]{1,0:T(1,128)S(1)}, f32[1,256]{1,0:T(1,128)S(1)}) all-reduce(f32[1,256]{1,0:T(1,128)S(1)} %bitcast.214, f32[1,256]{1,0:T(1,128)S(1)} %bitcast.215), channel_id=1, replica_groups=mesh['seq'=16,'head'=8,'dp'=2] {'head'}, use_global_device_ids=true, to_apply=%region_1.0 | all-reduce | flops 512 | bytes 4096 | tf_op jit(solution)/shard_map/psum | solution.py:43
  33.3 1.3 multiply_reduce_fusion.1
  34.6 42.1 %all-gather.3.cloned.1.call-done = bf16[1,1024,512]{2,1,0:T(8,128)(2,1)} async-done(((bf16[1,64,512]{2,1,0:T(8,128)(2,1)}), bf16[1,1024,512]{2,1,0:T(8,128)(2,1)}) %all-gather.3.cloned.1.call-update) | async-done | bytes 1048592 | tf_op jit(solution)/shard_map/all_gather | solution.py:120
  76.7 49.9 %all-gather.5.cloned.1.call-done = bf16[1,1024,512]{2,1,0:T(8,128)(2,1)} async-done(((bf16[1,64,512]{2,1,0:T(8,128)(2,1)}), bf16[1,1024,512]{2,1,0:T(8,128)(2,1)}) %all-gather.5.cloned.1.call-update) | async-done | bytes 1048592 | tf_op jit(solution)/shard_map/all_gather | solution.py:121
  126.7 2.4 conditional.3
  127.5 1.6 broadcast_in_dim.26
  129.1 6.2 %copy.113 = bf16[2,1,1024,512]{3,0,1,2:T(2,128)(2,1)} copy(bf16[2,1,1024,512]{2,3,1,0:T(8,128)(2,1)} %get-tuple-element.81) | data formatting | bytes 4194304 | tf_op jit(solution)/shard_map/cond | solution.py:155
  137.9 2.0 copy.121
  140.1 1.3 convolution_multiply_fusion.3
  141.7 1.4 fusion.29
  143.5 119.0 %all-reduce.8.cloned.1.call-done = bf16[2,1,1024,512]{3,0,1,2:T(2,128)(2,1)} async-done(((bf16[2,1,1024,512]{3,0,1,2:T(2,128)(2,1)}), bf16[2,1,1024,512]{3,0,1,2:T(2,128)(2,1)}) %all-reduce.8.cloned.1.call-update) | async-done | bytes 2097168
  262.5 1.7 dynamic-slice_reduce_fusion
  264.2 1.1 convolution_convert_fusion.1
  266.4 1.2 fusion.27
  267.6 1.2 reshape.534
  269.9 1.3 reshape.535
  271.4 13.9 %all-reduce.1 = (f32[256]{0:T(256)S(1)}, f32[256]{0:T(256)S(1)}) all-reduce(f32[256]{0:T(256)S(1)} %get-tuple-element.163, f32[256]{0:T(256)S(1)} %get-tuple-element.159), channel_id=1, replica_groups=mesh['seq'=16,'head'=8,'dp'=2] {'head'}, use_global_device_ids=true, to_apply=%region_15.16 | all-reduce | flops 512 | bytes 4096 | tf_op jit(solution)/shard_map/psum | solution.py:191
  287.3 67.7 %all-reduce.3 = (bf16[512]{0:T(512)(128)(2,1)S(1)}, bf16[512]{0:T(512)(128)(2,1)S(1)}) all-reduce(bf16[512]{0:T(512)(128)(2,1)S(1)} %get-tuple-element.162, bf16[512]{0:T(512)(128)(2,1)S(1)} %get-tuple-element.158), channel_id=1, replica_groups=mesh['seq'=16,'head'=8,'dp'=2] {'seq','dp'}, use_global_device_ids=true, to_apply=%region_20.21 | all-reduce | flops 1024 | bytes 4096 | tf_op jit(solution)/shard_map/psum | solution.py:204
  356.2 1.2 reshape.538
  358.5 1.3 reshape.539
  361.4 26.2 %all-reduce.10.cloned.1.call-done = (bf16[4,512,128]{1,2,0:T(8,128)(2,1)}, bf16[4,512,128]{2,1,0:T(8,128)(2,1)}) async-done(((bf16[4,512,128]{1,2,0:T(8,128)(2,1)}, bf16[4,512,128]{2,1,0:T(8,128)(2,1)}), (bf16[4,512,128]{1,2,0:T(8,128)(2,1)}, bf16[4,512,128]{2,1,0:T(8,128)(2,1)})) %all-reduce.10.cloned.1.call-update) | async-done | bytes 1048592 | tf_op jit(solution)/shard_map/psum | solution.py:207
  387.7 2.2 copy.125
  389.9 2.1 convert_element_type.123
  (84 shorter events, 19.5 us)
Async XLA Ops:
  7.2 21.1 %copy-start = (bf16[4,512,128]{2,1,0:T(8,128)(2,1)S(1)}, bf16[4,512,128]{2,1,0:T(8,128)(2,1)}, u32[]{:S(2)}) copy-start(bf16[4,512,128]{2,1,0:T(8,128)(2,1)} %param.17) | copy-start | bytes 1572868
  7.2 24.3 %copy-start.1 = (bf16[1,256,512]{2,1,0:T(8,128)(2,1)S(1)}, bf16[1,256,512]{2,1,0:T(8,128)(2,1)}, u32[]{:S(2)}) copy-start(bf16[1,256,512]{2,1,0:T(8,128)(2,1)} %param.12) | copy-start | bytes 786436
  7.2 24.8 %copy-start.16 = (bf16[1,256,512]{2,1,0:T(8,128)(2,1)S(1)}, bf16[1,256,512]{2,1,0:T(8,128)(2,1)}, u32[]{:S(2)}) copy-start(bf16[1,256,512]{2,1,0:T(8,128)(2,1)} %param.14) | copy-start | bytes 786436
  7.2 23.3 %copy-start.11 = (bf16[4,512,128]{2,1,0:T(8,128)(2,1)S(1)}, bf16[4,512,128]{2,1,0:T(8,128)(2,1)}, u32[]{:S(2)}) copy-start(bf16[4,512,128]{2,1,0:T(8,128)(2,1)} %param.18) | copy-start | bytes 1572868
  7.2 24.2 %copy-start.18 = (f32[512]{0:T(512)S(1)}, f32[512]{0:T(512)}, u32[]{:S(2)}) copy-start(f32[512]{0:T(512)} %param.15) | copy-start | bytes 6148
  7.2 69.5 %all-gather.3.cloned.1.call-start = ((), (), s32[]{:S(2)}) async-start(), calls=%async_computation | async-start | bytes 1114112 | tf_op jit(solution)/shard_map/all_gather | solution.py:120
  26.8 5.9 %copy-start.17 = (bf16[1,256,512]{2,1,0:T(8,128)(2,1)S(1)}, bf16[1,256,512]{2,1,0:T(8,128)(2,1)}, u32[]{:S(2)}) copy-start(bf16[1,256,512]{2,1,0:T(8,128)(2,1)} %param.19) | copy-start | bytes 786436
  28.3 4.7 %copy-start.6 = (bf16[64,4,512]{2,0,1:T(8,128)(2,1)}, bf16[64,4,512]{2,0,1:T(8,128)(2,1)S(1)}, u32[]{:S(2)}) copy-start(bf16[64,4,512]{2,0,1:T(8,128)(2,1)S(1)} %reshape.525) | copy-start | bytes 786436
  29.2 97.5 %all-gather.5.cloned.1.call-start = ((), (), s32[]{:S(2)}) async-start(), calls=%async_computation.1 | async-start | bytes 1114112 | tf_op jit(solution)/shard_map/all_gather | solution.py:121
  30.5 2.5 copy-start.8
  31.4 231.1 %all-reduce.8.cloned.1.call-start = ((), (), s32[]{:S(2)}) async-start(), calls=%async_computation.2 | async-start | bytes 4194304
  31.8 1.5 copy-start.5
  32.0 1.4 copy-start.4
  129.1 6.4 %copy-start.20 = (u32[256]{0:T(256)S(1)}, u32[256]{0:T(256)}, u32[]{:S(2)}) copy-start(u32[256]{0:T(256)} %constant.48) | copy-start | bytes 3076
  135.3 252.4 %all-reduce.10.cloned.1.call-start = ((), (), s32[]{:S(2)}) async-start(), calls=%async_computation.3 | async-start | bytes 2097152 | tf_op jit(solution)/shard_map/psum | solution.py:207
  140.1 124.0 %copy-start.7 = (bf16[64,4,512]{2,0,1:T(8,128)(2,1)S(1)}, bf16[64,4,512]{2,0,1:T(8,128)(2,1)}, u32[]{:S(2)}) copy-start(bf16[64,4,512]{2,0,1:T(8,128)(2,1)} %copy-done.6) | copy-start | bytes 786436
  140.1 126.3 %copy-start.9 = (bf16[64,4,512]{2,0,1:T(8,128)(2,1)S(1)}, bf16[64,4,512]{2,0,1:T(8,128)(2,1)}, u32[]{:S(2)}) copy-start(bf16[64,4,512]{2,0,1:T(8,128)(2,1)} %copy-done.8) | copy-start | bytes 786436
  143.2 127.9 %copy-start.3 = (bf16[1,256,512]{2,1,0:T(8,128)(2,1)S(1)}, bf16[1,256,512]{2,1,0:T(8,128)(2,1)}, u32[]{:S(2)}) copy-start(bf16[1,256,512]{2,1,0:T(8,128)(2,1)} %param.13) | copy-start | bytes 786436
  143.3 127.9 %copy-start.19 = (f32[512]{0:T(512)S(1)}, f32[512]{0:T(512)}, u32[]{:S(2)}) copy-start(f32[512]{0:T(512)} %param.16) | copy-start | bytes 6148
  265.3 20.9 %copy-start.12 = (bf16[4,512,128]{2,1,0:T(8,128)(2,1)S(1)}, bf16[4,512,128]{2,1,0:T(8,128)(2,1)}, u32[]{:S(2)}) copy-start(bf16[4,512,128]{2,1,0:T(8,128)(2,1)} %param.18) | copy-start | bytes 1572868
  286.2 73.5 %copy-start.13 = (f32[1,256,512]{2,1,0:T(8,128)S(1)}, f32[1,256,512]{2,1,0:T(8,128)}, u32[]{:S(2)}) copy-start(f32[1,256,512]{2,1,0:T(8,128)} %copy.121) | copy-start | bytes 1572868
Sparse Core Ops, SparseCore 0:
  29.3 47.3 all-gather.2
  79.7 46.8 all-gather.4
  135.4 127.0 all-reduce.7
  271.3 116.3 all-reduce.9
where the time goes:
time: 399 us; the launch traced here: 398 us
  waiting for transfers between devices  237 us (59%)
  blocking collectives  98.8 us (25%)
  local copies, waits for them, and re-layouts  26.8 us (7%)
  between operations  14.8 us (4%)
  matrix products  10.3 us (3%)
  other arithmetic  10.1 us (3%)
    unnamed x5, waiting for transfers between devices  119 us
    psum x1, blocking collectives, on_device(): lax.psum(gain_q_part.astype(jnp.bfloat16), ('seq', 'dp'))  67.7 us
    all_gather x1, waiting for transfers between devices, on_device(): lax.all_gather(mem_v, 'seq', axis=1, tiled=True)  49.9 us
    all_gather x1, waiting for transfers between devices, on_device(): lax.all_gather(mem_k, 'seq', axis=1, tiled=True)  42.1 us
    psum x1, waiting for transfers between devices, on_device(): lax.psum(squeeze_v_part.astype(jnp.bfloat16), ('seq', 'dp'))  26.2 us
    psum x1, blocking collectives, on_device(): lax.psum((jnp.sum(q_full * q_full, -1), jnp.sum(k_full * k_full, -1)), 'h...  17.3 us
    psum x1, blocking collectives, on_device(): lax.psum((jnp.sum(query_gain * grad_qn * q_full, -1), jnp.sum(key_gain *...  13.9 us
  transfers between devices with their start and end apart: 4, of which 4 were waited for; matrix products, arithmetic and copies ran while one was open for 5% of the time, Pallas kernels for 0%

commit v1 on v0

v1 whole, which is shorter than its diff:
```python
import functools

import jax
import jax.numpy as jnp
from jax import lax
from jax.experimental import pallas as pl
from jax.experimental.pallas import tpu as pltpu
from jax.sharding import PartitionSpec as P

HD = 128
KS = 4
N = 4
T = 256
M = 64
EPS = 1e-06
NEG = -1e30
MESH = pl.DeviceIdType.MESH
F32 = jnp.float32
BF16 = jnp.bfloat16
PIECE = 144

A2A = 0
Z1 = A2A + 12
Y1 = Z1 + 7
MEM = Y1 + 3
DMEM = MEM + 6
DQ = DMEM + 24
DK = DQ + 3
DV = DK + 3
PD = DV + 3
Z2 = PD + 3
C1 = Z2 + 7
RS = C1 + 1
AGX = RS + 3
AGY = AGX + 3
C2 = AGY + 3
N_SEM = C2 + 4


def dot_nt(a, b):
    return lax.dot_general(a, b, (((1,), (1,)), ((), ())), preferred_element_type=F32)


def dot_tn(a, b):
    return lax.dot_general(a, b, (((0,), (0,)), ((), ())), preferred_element_type=F32)


def dot_nn(a, b):
    return lax.dot_general(a, b, (((1,), (0,)), ((), ())), preferred_element_type=F32)


def as_column(row):
    return jnp.transpose(jnp.broadcast_to(row, (HD, row.shape[1])))


def row_sum(block):
    return jnp.sum(jnp.transpose(block), 0, keepdims=True)


def fold8(block):
    return block.reshape(block.shape[0] // 8, 8, block.shape[1])


def kernel(
    nz,
    q_ref, k_ref, v_ref, o_ref, gq_ref, gk_ref, wk_ref, wv_ref,
    dq_out, dk_out, dv_out, qg_out, kg_out, sk_out, sv_out,
    hq, hk, hv, ho, qn, kn, icq, ick, fs, ku, vu, zs, ys, mk, mv,
    s_all, g_all, d_buf, p_buf, dmk, dmv, sbk, sbv, rbk, rbv,
    dkl, dvl, aq, ak, av, pd, aqh, akh, avh, pdh, zs2,
    pay, pin, rsb, rsi, full,
    ss, rs, loc,
):
    seq = lax.axis_index("seq")
    x = lax.rem(seq, N)
    y = lax.div(seq, N)
    z = lax.axis_index("head")
    c = lax.axis_index("dp")
    hh = nz * N * HD
    scale = HD ** (-0.5)

    def ydev(r):
        return {"seq": lax.rem(y + r, N) * N + x}

    def xdev(r):
        return {"seq": y * N + lax.rem(x + r, N)}

    def zdev(r):
        return {"head": lax.rem(z + r, nz)}

    cdev = {"dp": 1 - c}

    def remote(src, dst, index, device):
        return pltpu.make_async_remote_copy(
            src_ref=src,
            dst_ref=dst,
            send_sem=ss.at[index],
            recv_sem=rs.at[index],
            device_id=device,
            device_id_type=MESH,
        )

    sent = []

    def start(copy):
        copy.start()
        sent.append(copy)
        return copy

    barrier = pltpu.get_barrier_semaphore()
    peers = [ydev(r) for r in (1, 2, 3)] + [xdev(r) for r in (1, 2, 3)]
    peers += [zdev(r) for r in range(1, nz)] + [cdev]
    for peer in peers:
        pl.semaphore_signal(barrier, inc=1, device_id=peer, device_id_type=MESH)

    for row, ref in ((0, q_ref), (1, k_ref)):
        full_rows = ref[...].astype(F32)
        squares = full_rows * full_rows
        folded = squares[:, :HD]
        for h in range(1, N):
            folded = folded + squares[:, h * HD : (h + 1) * HD]
        zs[z, row : row + 1, :] = row_sum(folded)

    pl.semaphore_wait(barrier, len(peers))

    z1 = [start(remote(zs.at[z], zs.at[z], Z1 + r - 1, zdev(r))) for r in range(1, nz)]
    rows_mine = pl.ds(pl.multiple_of(y * T, T), T)
    a2a = []
    own = []
    for i, (src, dst) in enumerate(((v_ref, hv), (k_ref, hk), (q_ref, hq), (o_ref, ho))):
        group = []
        for r in (1, 3, 2):
            cols = pl.ds(pl.multiple_of(lax.rem(y + r, N) * HD, HD), HD)
            group.append(
                start(remote(src.at[:, cols], dst.at[rows_mine, :], A2A + 3 * i + r - 1, ydev(r)))
            )
        a2a.append(group)
        cols = pl.ds(pl.multiple_of(y * HD, HD), HD)
        copy = pltpu.make_async_copy(src.at[:, cols], dst.at[rows_mine, :], loc.at[i])
        copy.start()
        own.append(copy)

    def arrived(i):
        for copy in a2a[i]:
            copy.wait_recv()
        own[i].wait()

    for copy in z1:
        copy.wait_recv()
    total = zs[0]
    for r in range(1, nz):
        total = total + zs[r]
    ys[y] = total
    y1 = [start(remote(ys.at[y], ys.at[y], Y1 + r - 1, ydev(r))) for r in (1, 3, 2)]

    def unfold(dst):
        for j in range(KS):
            dst[:, j * HD : (j + 1) * HD] = fs[pl.ds(j, N * M, stride=KS), :].astype(BF16)

    def spread(mem, value, index):
        rounded = value.astype(BF16)
        for b in range(N):
            mem[b, x] = rounded[b * M : (b + 1) * M]
        return [
            start(remote(mem.at[:, x], mem.at[:, x], MEM + 3 * index + r - 1, xdev(r)))
            for r in (1, 3, 2)
        ]

    arrived(0)
    fs[...] = hv[...].astype(F32)
    unfold(vu)
    mem_copies = spread(mv, dot_nn(vu[...], wv_ref[y]), 1)

    for copy in y1:
        copy.wait_recv()
    gain_q = gq_ref[y]
    gain_k = gk_ref[y]
    arrived(1)
    for a in range(N):
        rows = slice(a * T, (a + 1) * T)
        inverse = lax.rsqrt(ys[a] * (1.0 / hh) + EPS)
        icq[rows, :] = as_column(inverse[0:1])
        ick[rows, :] = as_column(inverse[1:2])
        normed = (hk[rows, :].astype(F32) * ick[rows, :] * gain_k).astype(BF16)
        kn[rows, :] = normed
        fs[rows, :] = normed.astype(F32)
    unfold(ku)
    mem_copies += spread(mk, dot_nn(ku[...], wk_ref[y]), 0)

    arrived(2)
    arrived(3)
    key_at = lax.broadcasted_iota(jnp.int32, (T, T), 0)
    query_at = lax.broadcasted_iota(jnp.int32, (T, T), 1)
    peaks = []
    for a in range(N):
        rows = slice(a * T, (a + 1) * T)
        normed = (hq[rows, :].astype(F32) * icq[rows, :] * gain_q).astype(BF16)
        qn[rows, :] = normed
        scores = jnp.where(key_at <= query_at, dot_nt(kn[rows, :], normed), NEG)
        s_all[a, 0:T, :] = scores
        g_all[a, 0:T, :] = dot_nt(hv[rows, :], ho[rows, :])
        peaks.append(jnp.max(fold8(scores), 0))

    for copy in mem_copies:
        copy.wait_recv()

    gain_q_sum = jnp.zeros((8, HD), F32)
    dmem_copies = []
    for a in range(N - 1, -1, -1):
        rows = slice(a * T, (a + 1) * T)
        width = T * (a + 2)
        q_rows = qn[rows, :]
        o_rows = ho[rows, :]
        peak8 = peaks[a]
        for b in range(a + 1):
            scores = dot_nt(mk[b].reshape(T, HD), q_rows)
            if b == a:
                scores = jnp.where(key_at < x * M, scores, NEG)
            at = slice(T * (b + 1), T * (b + 2))
            s_all[a, at, :] = scores
            peak8 = jnp.maximum(peak8, jnp.max(fold8(scores), 0))
            g_all[a, at, :] = dot_nt(mv[b].reshape(T, HD), o_rows)
        peak = jnp.max(peak8, 0, keepdims=True)

        def lift(i, state, a=a, peak=peak):
            mass8, weighted8 = state
            at = pl.ds(pl.multiple_of(i * 64, 64), 64)
            lifted = jnp.exp((s_all[a, at, :] - peak) * scale)
            s_all[a, at, :] = lifted
            mass8 = mass8 + jnp.sum(fold8(lifted), 0)
            weighted8 = weighted8 + jnp.sum(fold8(lifted * g_all[a, at, :]), 0)
            return mass8, weighted8

        none = jnp.zeros((8, T), F32)
        mass8, weighted8 = lax.fori_loop(0, width // 64, lift, (none, none))
        inverse_mass = 1.0 / jnp.sum(mass8, 0, keepdims=True)
        row_delta = jnp.sum(weighted8, 0, keepdims=True) * inverse_mass

        def settle(i, state, a=a, inverse_mass=inverse_mass, row_delta=row_delta):
            at = pl.ds(pl.multiple_of(i * 64, 64), 64)
            attend = s_all[a, at, :] * inverse_mass
            p_buf[at, :] = attend.astype(BF16)
            d_buf[at, :] = (attend * (g_all[a, at, :] - row_delta)).astype(BF16)
            return state

        lax.fori_loop(0, width // 64, settle, 0)

        for b in range(a, -1, -1):
            at = slice(T * (b + 1), T * (b + 2))
            add_k = dot_nn(d_buf[at, :], q_rows)
            add_v = dot_nn(p_buf[at, :], o_rows)
            if a < N - 1:
                add_k = add_k + dmk[b * T : (b + 1) * T, :]
                add_v = add_v + dmv[b * T : (b + 1) * T, :]
            if b == a:
                sbk[a] = (add_k * scale).astype(BF16).reshape(N, M, HD)
                sbv[a] = add_v.astype(BF16).reshape(N, M, HD)
                for i, (sb, rb) in enumerate(((sbk, rbk), (sbv, rbv))):
                    for r in (1, 3, 2):
                        to = lax.rem(x + r, N)
                        index = DMEM + 12 * i + 3 * a + r - 1
                        dmem_copies.append(
                            start(remote(sb.at[a, to], rb.at[x, a], index, xdev(r)))
                        )
            else:
                dmk[b * T : (b + 1) * T, :] = add_k
                dmv[b * T : (b + 1) * T, :] = add_v
        grad_q = dot_tn(d_buf[0:T, :], kn[rows, :])
        for b in range(a + 1):
            at = slice(T * (b + 1), T * (b + 2))
            grad_q = grad_q + dot_tn(d_buf[at, :], mk[b].reshape(T, HD))
        grad_q = grad_q * scale
        dkl[rows, :] = dot_nn(d_buf[0:T, :], q_rows) * scale
        dvl[rows, :] = dot_nn(p_buf[0:T, :], o_rows)
        q_full = hq[rows, :].astype(F32)
        inv = icq[rows, :]
        gain_q_sum = gain_q_sum + jnp.sum(fold8(grad_q * q_full * inv), 0)
        gained = grad_q * gain_q
        aq[a] = (gained * inv).astype(BF16)
        pd[a, 0:1, :] = row_sum(gained * q_full)

    def homeward(src, dst, base):
        dst[y] = src[y]
        return [
            start(remote(src.at[lax.rem(y + r, N)], dst.at[y], base + r - 1, ydev(r)))
            for r in (1, 3, 2)
        ]

    home = homeward(aq, aqh, DQ)

    for copy in dmem_copies:
        copy.wait_recv()
    grad_mem_k = []
    grad_mem_v = []
    for out, sb, rb in ((grad_mem_k, sbk, rbk), (grad_mem_v, sbv, rbv)):
        for b in range(N):
            total = sb[b, x].astype(F32)
            for r in (1, 2, 3):
                total = total + rb[lax.rem(x + r, N), b].astype(F32)
            out.append(total.astype(BF16))
    grad_mem_k = jnp.concatenate(grad_mem_k, 0)
    grad_mem_v = jnp.concatenate(grad_mem_v, 0)

    square_k = dot_tn(ku[...], grad_mem_k)
    square_v = dot_tn(vu[...], grad_mem_v)
    for p in range(N):
        pay[0, p, 0:HD, :] = square_k[p * HD : (p + 1) * HD].astype(BF16)
        pay[1, p, 0:HD, :] = square_v[p * HD : (p + 1) * HD].astype(BF16)
    for j in range(KS):
        at = pl.ds(j, N * M, stride=KS)
        cols = slice(j * HD, (j + 1) * HD)
        dkl[at, :] = dkl[at, :] + dot_nt(grad_mem_k, wk_ref[y, cols, :])
        dvl[at, :] = dvl[at, :] + dot_nt(grad_mem_v, wv_ref[y, cols, :])
    gain_k_sum = jnp.zeros((8, HD), F32)
    for a in range(N):
        rows = slice(a * T, (a + 1) * T)
        av[a] = dvl[rows, :].astype(BF16)
        grad_k = dkl[rows, :]
        k_full = hk[rows, :].astype(F32)
        inv = ick[rows, :]
        gain_k_sum = gain_k_sum + jnp.sum(fold8(grad_k * k_full * inv), 0)
        gained = grad_k * gain_k
        ak[a] = (gained * inv).astype(BF16)
        pd[a, 1:2, :] = row_sum(gained * k_full)
    tail = PIECE - HD
    tail_k = jnp.broadcast_to(jnp.sum(gain_k_sum, 0, keepdims=True), (tail, HD)).astype(BF16)
    tail_q = jnp.broadcast_to(jnp.sum(gain_q_sum, 0, keepdims=True), (tail, HD)).astype(BF16)
    for p in range(N):
        pay[0, p, HD:PIECE, :] = tail_k
        pay[1, p, HD:PIECE, :] = tail_q

    c1 = start(remote(pay.at[1 - c], pin, C1, cdev))
    home_pd = homeward(pd, pdh, PD)
    home += homeward(ak, akh, DK)
    home += homeward(av, avh, DV)

    c1.wait_recv()
    for p in range(N):
        rsb[p] = (pay[c, p].astype(F32) + pin[p].astype(F32)).astype(BF16)
    rs_copies = [
        start(remote(rsb.at[lax.rem(x + r, N)], rsi.at[x], RS + r - 1, xdev(r)))
        for r in (1, 3, 2)
    ]

    for copy in home_pd:
        copy.wait_recv()
    total = pdh[0]
    for h in range(1, N):
        total = total + pdh[h]
    zs2[z] = total
    z2 = [start(remote(zs2.at[z], zs2.at[z], Z2 + r - 1, zdev(r))) for r in range(1, nz)]

    for copy in rs_copies:
        copy.wait_recv()
    total = rsb[x].astype(F32)
    for r in (1, 2, 3):
        total = total + rsi[lax.rem(x + r, N)].astype(F32)
    full[c, y, x] = total.astype(BF16)
    agx = [
        start(remote(full.at[c, y, x], full.at[c, y, x], AGX + r - 1, xdev(r))) for r in (1, 3, 2)
    ]
    for copy in agx:
        copy.wait_recv()
    agy = [start(remote(full.at[c, y], full.at[c, y], AGY + r - 1, ydev(r))) for r in (1, 3, 2)]
    c2 = [start(remote(full.at[c, y], full.at[c, y], C2, cdev))]

    for copy in z2:
        copy.wait_recv()
    total = zs2[0]
    for r in range(1, nz):
        total = total + zs2[r]
    inverse = lax.rsqrt(ys[y] * (1.0 / hh) + EPS)
    shift = inverse * inverse * inverse * total * (1.0 / hh)
    shift_q = as_column(shift[0:1])
    shift_k = as_column(shift[1:2])
    for copy in home:
        copy.wait_recv()
    for h in range(N):
        cols = slice(h * HD, (h + 1) * HD)
        dq_out[:, cols] = (aqh[h].astype(F32) - q_ref[:, cols].astype(F32) * shift_q).astype(BF16)
        dk_out[:, cols] = (akh[h].astype(F32) - k_ref[:, cols].astype(F32) * shift_k).astype(BF16)
        dv_out[:, cols] = avh[h]

    for i, r in enumerate((1, 3, 2)):
        agy[i].wait_recv()
        at = full.at[c, lax.rem(y + N - r, N)]
        c2.append(start(remote(at, at, C2 + i + 1, cdev)))
    for copy in c2:
        copy.wait_recv()
    for h in range(N):
        for p in range(N):
            rows = slice(p * HD, (p + 1) * HD)
            sk_out[h, rows, :] = full[0, h, p, 0:HD, :].astype(F32)
            sv_out[h, rows, :] = full[1, h, p, 0:HD, :].astype(F32)
        kg_out[h] = full[0, h, 0, HD:PIECE, :].astype(F32)[0:1]
        qg_out[h] = full[1, h, 0, HD:PIECE, :].astype(F32)[0:1]

    for copy in sent:
        copy.wait_send()


def on_device(nz, q, k, v, query_gain, key_gain, key_squeeze, value_squeeze, o):
    width = N * HD
    bf = functools.partial(pltpu.VMEM, dtype=BF16)
    ff = functools.partial(pltpu.VMEM, dtype=F32)
    rows = N * T
    scratch = [bf((rows, HD))] * 4 + [bf((rows, HD))] * 2 + [ff((rows, HD))] * 2
    scratch += [ff((rows, HD)), bf((N * M, KS * HD)), bf((N * M, KS * HD))]
    scratch += [ff((nz, 2, T)), ff((N, 2, T)), bf((N, N, M, HD)), bf((N, N, M, HD))]
    deep = (N + 1) * T
    scratch += [ff((N, deep, T)), ff((N, deep, T)), bf((deep, T)), bf((deep, T))]
    scratch += [ff((N * T, HD))] * 2 + [bf((N, N, M, HD))] * 4
    scratch += [ff((rows, HD))] * 2 + [bf((N, T, HD))] * 3 + [ff((N, 2, T))]
    scratch += [bf((N, T, HD))] * 3 + [ff((N, 2, T)), ff((nz, 2, T))]
    scratch += [bf((2, N, PIECE, HD)), bf((N, PIECE, HD)), bf((N, PIECE, HD))]
    scratch += [bf((N, PIECE, HD)), bf((2, N, N, PIECE, HD))]
    scratch += [
        pltpu.SemaphoreType.DMA((N_SEM,)),
        pltpu.SemaphoreType.DMA((N_SEM,)),
        pltpu.SemaphoreType.DMA((4,)),
    ]
    vmem = pl.BlockSpec(memory_space=pltpu.VMEM)
    outs = pl.pallas_call(
        functools.partial(kernel, nz),
        out_shape=[jax.ShapeDtypeStruct((T, width), BF16)] * 3
        + [jax.ShapeDtypeStruct((N, 1, HD), F32)] * 2
        + [jax.ShapeDtypeStruct((N, KS * HD, HD), F32)] * 2,
        in_specs=[vmem] * 8,
        out_specs=[vmem] * 7,
        scratch_shapes=scratch,
        compiler_params=pltpu.CompilerParams(
            collective_id=0, has_side_effects=True, vmem_limit_bytes=60 * 2**20
        ),
    )(
        q[0], k[0], v[0], o[0],
        query_gain.reshape(N, 1, HD), key_gain.reshape(N, 1, HD),
        key_squeeze, value_squeeze,
    )
    dq, dk, dv, qg, kg, sk, sv = outs
    return dq[None], dk[None], dv[None], qg.reshape(width), kg.reshape(width), sk, sv


def solution(mesh):
    by_token = P("dp", "seq", "head")
    by_head = P("head", None, None)
    return jax.shard_map(
        functools.partial(on_device, mesh.shape["head"]),
        mesh=mesh,
        in_specs=(by_token,) * 3 + (P("head"), P("head"), by_head, by_head, by_token),
        out_specs=(by_token,) * 3 + (P("head"), P("head"), by_head, by_head),
        check_vma=False,
    )
```

time: 399 us -> 73.4 us (0.18)
  waiting for transfers between devices: 237 us -> 0 us
  blocking collectives: 98.8 us -> 0 us
  Pallas kernels: 0 us -> 63.6 us
  local copies, waits for them, and re-layouts: 26.8 us -> 8.93 us
  between operations: 14.8 us -> 0.66 us
  matrix products: 10.3 us -> 0 us
  other arithmetic: 10.1 us -> 0 us
    unnamed x5 -> x0, waiting for transfers between devices: 119 us -> none
    psum x3 -> x0, blocking collectives: 98.8 us -> none  [the longest x1 67.7 us: on_device(): lax.psum(gain_q_part.astype(jnp.bfloat16), ('seq', 'dp'))]
    all_gather x2 -> x0, waiting for transfers between devices: 92 us -> none  [the longest x1 49.9 us: on_device(): lax.all_gather(mem_v, 'seq', axis=1, tiled=True)]
    pallas_call x0 -> x1, Pallas kernels: none -> 63.6 us  [on_device(): pl.pallas_call(functools.partial(kernel, nz), out_shape=[jax.ShapeDtypeSt...]
    psum x1 -> x0, waiting for transfers between devices: 26.2 us -> none  [on_device(): lax.psum(squeeze_v_part.astype(jnp.bfloat16), ('seq', 'dp'))]
    dot_general x11 -> x0, matrix products: 10.3 us -> none  [the longest x1 1.36 us: on_device(): jnp.einsum('bhtu,buhd->bthd', d_loc, key_loc, preferred_element_type=jnp....]
    reshape x12 -> x0, local copies, waits for them, and re-layouts: 9.78 us -> none  [the longest x2 2.5 us: fold_slots(): return source.reshape(batch_size, slot_count, head_count, KS, HD).transpo...]
    convert_element_type x9 -> x0, other arithmetic: 7.29 us -> none  [the longest x1 2.08 us: on_device(): lax.psum(squeeze_k_part.astype(jnp.bfloat16), ('seq', 'dp'))]
  transfers between devices with their start and end apart: 4 -> 0, of which waited for: 4 -> 0; matrix products, arithmetic and copies ran while one was open for 5% -> 0% of each run, Pallas kernels for 0% -> 0%
where the time goes in v1:
time: 73.4 us; the launch traced here: 73.2 us
  Pallas kernels  63.6 us (87%)
  local copies, waits for them, and re-layouts  8.93 us (12%)
    pallas_call x1, Pallas kernels, on_device(): pl.pallas_call(functools.partial(kernel, nz), out_shape=[jax.ShapeDtypeSt...  63.6 us
    unnamed x15, local copies, waits for them, and re-layouts  8.93 us

profile of v1, /device:TPU:1, one launch (start us, length us, event | category | flops | bytes accessed | tf_op | source)
XLA Modules:
  0.0 73.2 jit_solution(3365592218822025595)
XLA Ops:
  0.6 63.6 %shard_map.135 = (bf16[256,512]{1,0:T(8,128)(2,1)}, bf16[256,512]{1,0:T(8,128)(2,1)}, bf16[256,512]{1,0:T(8,128)(2,1)}, f32[4,1,128]{2,1,0:T(1,128)}, f32[4,1,12...) custom-call(bf16[256,512]{1,0:T(8,128)(2,1)} %bitcast.14, bf16[256,512]{1,0:T(8,128)(2,1)} %bitcast.15, ...), custom_call_target="tpu_custom_call" | custom-call | tf_op jit(solution)/shard_map/pallas_call | solution.py:423
  64.2 0.0 copy-start.1
  64.3 1.8 %copy.22 = bf16[1,256,512]{2,1,0:T(8,128)(2,1)} copy(bf16[1,256,512]{2,1,0:T(8,128)(2,1)} %bitcast.13) | data formatting | bytes 524288
  66.0 1.7 %copy.23 = bf16[1,256,512]{2,1,0:T(8,128)(2,1)} copy(bf16[1,256,512]{2,1,0:T(8,128)(2,1)} %bitcast.12) | data formatting | bytes 524288
  67.7 0.0 copy-start.3
  67.7 1.7 %copy.24 = bf16[1,256,512]{2,1,0:T(8,128)(2,1)} copy(bf16[1,256,512]{2,1,0:T(8,128)(2,1)} %bitcast.11) | data formatting | bytes 524288
  69.4 0.0 copy-done.3
  69.4 0.0 copy-start.2
  69.4 0.6 copy.25
  69.9 0.1 copy-done.2
  70.0 0.6 copy.26
  70.6 0.0 copy-done.1
  70.6 0.0 copy-start
  70.6 1.0 %copy.27 = f32[4,512,128]{2,1,0:T(8,128)} copy(f32[4,512,128]{2,1,0:T(8,128)S(1)} %copy-done.1) | data formatting | bytes 2097152
  71.6 0.6 copy-done
  72.2 1.0 %copy.28 = f32[4,512,128]{2,1,0:T(8,128)} copy(f32[4,512,128]{2,1,0:T(8,128)S(1)} %copy-done) | data formatting | bytes 2097152
Async XLA Ops:
  64.2 6.4 %copy-start.1 = (f32[4,512,128]{2,1,0:T(8,128)S(1)}, f32[4,512,128]{2,1,0:T(8,128)}, u32[]{:S(2)}) copy-start(f32[4,512,128]{2,1,0:T(8,128)} %get-tuple-element.33) | copy-start | bytes 3145732
  67.7 1.7 %copy-start.3 = (f32[4,1,128]{2,1,0:T(1,128)S(1)}, f32[4,1,128]{2,1,0:T(1,128)}, u32[]{:S(2)}) copy-start(f32[4,1,128]{2,1,0:T(1,128)} %get-tuple-element.17) | copy-start | bytes 6148
  69.4 0.7 copy-start.2
  70.6 1.6 %copy-start = (f32[4,512,128]{2,1,0:T(8,128)S(1)}, f32[4,512,128]{2,1,0:T(8,128)}, u32[]{:S(2)}) copy-start(f32[4,512,128]{2,1,0:T(8,128)} %get-tuple-element.34) | copy-start | bytes 3145732

commit v2 on v1

v2 whole, which is shorter than its diff:
```python
import functools

import jax
import jax.numpy as jnp
from jax import lax
from jax.experimental import pallas as pl
from jax.experimental.pallas import tpu as pltpu
from jax.sharding import PartitionSpec as P

HD = 128
KS = 4
N = 4
T = 256
M = 64
EPS = 1e-06
NEG = -1e30
MESH = pl.DeviceIdType.MESH
F32 = jnp.float32
BF16 = jnp.bfloat16
PIECE = 144

A2A = 0
Z1 = A2A + 12
G1 = Z1 + 7
MEM = G1 + 3
DMEM = MEM + 6
DMEM1 = DMEM + 24
DQ = DMEM1 + 8
DK = DQ + 3
DV = DK + 3
PD = DV + 3
Z2 = PD + 3
RS = Z2 + 7
RSX = RS + 3
AGG = RSX + 4
AGO = AGG + 3
C2 = AGO + 3
N_SEM = C2 + 4


def dot_nt(a, b):
    return lax.dot_general(a, b, (((1,), (1,)), ((), ())), preferred_element_type=F32)


def dot_tn(a, b):
    return lax.dot_general(a, b, (((0,), (0,)), ((), ())), preferred_element_type=F32)


def dot_nn(a, b):
    return lax.dot_general(a, b, (((1,), (0,)), ((), ())), preferred_element_type=F32)


def as_column(row):
    return jnp.transpose(jnp.broadcast_to(row, (HD, row.shape[1])))


def row_sum(block):
    return jnp.sum(jnp.transpose(block), 0, keepdims=True)


def fold8(block):
    return block.reshape(block.shape[0] // 8, 8, block.shape[1])


def kernel(
    nz,
    q_hbm, k_hbm, v_hbm, o_hbm, gq_ref, gk_ref, wk_hbm, wv_hbm,
    dq_out, dk_out, dv_out, full_out,
    q_ref, k_ref, v_ref, o_ref, wk_ref, wv_ref,
    hq, hk, hv, ho, qn, kn, icq, ick, fs, ku, vu, zs, gs, mkg, mvg, mkc, mvc,
    s_all, g_all, d_all, p_all, acc_k, acc_v, sbk, sbv, rbk, rbv,
    dkl, dvl, aq, ak, av, pd, aqh, akh, avh, pdh, zs2,
    pay, rsi, full,
    ss, rs, loc,
):
    seq = lax.axis_index("seq")
    x = lax.rem(seq, N)
    y = lax.div(seq, N)
    z = lax.axis_index("head")
    c = lax.axis_index("dp")
    i = y + c * (x - y)
    j = x + c * (y - x)
    hh = nz * N * HD
    scale = HD ** (-0.5)
    first_core = c == 0

    def place(core, along, across):
        return along * (N - (N - 1) * core) + across * (1 + (N - 1) * core)

    def gdev(r):
        return {"seq": place(c, lax.rem(i + r, N), j)}

    def odev(r):
        return {"seq": place(c, i, lax.rem(j + r, N))}

    def cross(p):
        return {"seq": place(1 - c, i, p), "dp": 1 - c}

    def zdev(r):
        return {"head": lax.rem(z + r, nz)}

    cdev = {"dp": 1 - c}

    def remote(src, dst, index, device, landing=None):
        return pltpu.make_async_remote_copy(
            src_ref=src,
            dst_ref=dst,
            send_sem=ss.at[index],
            recv_sem=rs.at[index if landing is None else landing],
            device_id=device,
            device_id_type=MESH,
        )

    sent = []

    def start(copy):
        copy.start()
        sent.append((None, copy))
        return copy

    def start_if(cond, copy):
        pl.when(cond)(copy.start)
        sent.append((cond, copy))
        return copy

    barrier = pltpu.get_barrier_semaphore()
    peers = [gdev(r) for r in (1, 2, 3)] + [odev(r) for r in (1, 2, 3)]
    peers += [zdev(r) for r in range(1, nz)] + [cross(p) for p in range(N)] + [cdev]
    for peer in peers:
        pl.semaphore_signal(barrier, inc=1, device_id=peer, device_id_type=MESH)

    loads = [
        pltpu.make_async_copy(src, dst, loc.at[4 + n])
        for n, (src, dst) in enumerate(
            (
                (q_hbm, q_ref), (k_hbm, k_ref), (v_hbm, v_ref), (o_hbm, o_ref),
                (wv_hbm.at[i], wv_ref), (wk_hbm.at[i], wk_ref),
            )
        )
    ]
    for copy in loads:
        copy.start()

    for row, ref in ((0, q_ref), (1, k_ref)):
        loads[row].wait()
        full_rows = ref[...].astype(F32)
        squares = full_rows * full_rows
        folded = squares[:, :HD]
        for h in range(1, N):
            folded = folded + squares[:, h * HD : (h + 1) * HD]
        zs[z, row : row + 1, :] = row_sum(folded)
    for copy in loads[2:]:
        copy.wait()

    pl.semaphore_wait(barrier, len(peers))

    z1 = [start(remote(zs.at[z], zs.at[z], Z1 + r - 1, zdev(r))) for r in range(1, nz)]
    rows_mine = pl.ds(pl.multiple_of(i * T, T), T)
    a2a = {}

    def exchange(n, src, dst):
        group = []
        for r in (1, 3, 2):
            cols = pl.ds(pl.multiple_of(lax.rem(i + r, N) * HD, HD), HD)
            group.append(
                start(remote(src.at[:, cols], dst.at[rows_mine, :], A2A + 3 * n + r - 1, gdev(r)))
            )
        cols = pl.ds(pl.multiple_of(i * HD, HD), HD)
        copy = pltpu.make_async_copy(src.at[:, cols], dst.at[rows_mine, :], loc.at[n])
        copy.start()
        a2a[n] = (group, copy)

    def arrived(n):
        group, copy = a2a[n]
        for item in group:
            item.wait_recv()
        copy.wait()

    exchange(0, v_ref, hv)
    exchange(1, k_ref, hk)
    exchange(2, q_ref, hq)

    for copy in z1:
        copy.wait_recv()
    total = zs[0]
    for r in range(1, nz):
        total = total + zs[r]
    gs[i] = total
    g1 = [start(remote(gs.at[i], gs.at[i], G1 + r - 1, gdev(r))) for r in (1, 3, 2)]
    exchange(3, o_ref, ho)

    def unfold(dst):
        for n in range(KS):
            dst[:, n * HD : (n + 1) * HD] = fs[pl.ds(n, N * M, stride=KS), :].astype(BF16)

    mem_copies = []

    def spread(mem, value, index):
        mem[j] = value.astype(BF16).reshape(N, M, HD)
        for r in (1, 3, 2):
            wanted = first_core | (lax.rem(j + r, N) > j)
            copy = remote(mem.at[j], mem.at[j], MEM + 3 * index + r - 1, odev(r))
            start_if(wanted, copy)
            mem_copies.append((first_core | (lax.rem(j + N - r, N) < j), copy))

    arrived(0)
    fs[...] = hv[...].astype(F32)
    unfold(vu)
    spread(mvg, dot_nn(vu[...], wv_ref[...]), 1)

    for copy in g1:
        copy.wait_recv()
    gain_q = gq_ref[i]
    gain_k = gk_ref[i]
    arrived(1)
    for a in range(N):
        rows = slice(a * T, (a + 1) * T)
        inverse = lax.rsqrt(gs[a] * (1.0 / hh) + EPS)
        icq[rows, :] = as_column(inverse[0:1])
        ick[rows, :] = as_column(inverse[1:2])
        normed = (hk[rows, :].astype(F32) * ick[rows, :] * gain_k).astype(BF16)
        kn[rows, :] = normed
        fs[rows, :] = normed.astype(F32)
    unfold(ku)
    spread(mkg, dot_nn(ku[...], wk_ref[...]), 0)

    arrived(2)
    arrived(3)
    key_at = lax.broadcasted_iota(jnp.int32, (T, T), 0)
    query_at = lax.broadcasted_iota(jnp.int32, (T, T), 1)
    peaks = []
    for a in range(N):
        rows = slice(a * T, (a + 1) * T)
        normed = (hq[rows, :].astype(F32) * icq[rows, :] * gain_q).astype(BF16)
        qn[rows, :] = normed
        scores = jnp.where(key_at <= query_at, dot_nt(kn[rows, :], normed), NEG)
        s_all[a, 0:T, :] = scores
        g_all[a, 0:T, :] = dot_nt(hv[rows, :], ho[rows, :])
        peaks.append(jnp.max(fold8(scores), 0))

    for wanted, copy in mem_copies:
        pl.when(wanted)(copy.wait_recv)
    for b in range(N):
        for t in range(N):
            at = slice(t * M, (t + 1) * M)
            source = t + c * (b - t)
            member = b + c * (t - b)
            mkc[b, at, :] = mkg[source, member]
            mvc[b, at, :] = mvg[source, member]

    blocks = [a + c * (j - a) + 1 for a in range(N)]
    cuts = [M * (j + c * (a - j)) for a in range(N)]

    for a in range(N):
        rows = slice(a * T, (a + 1) * T)
        q_rows = qn[rows, :]
        o_rows = ho[rows, :]

        def score(b, peak8, a=a, q_rows=q_rows, o_rows=o_rows):
            limit = jnp.where(b == blocks[a] - 1, cuts[a], T)
            scores = jnp.where(key_at < limit, dot_nt(mkc[b], q_rows), NEG)
            at = pl.ds(pl.multiple_of(T * (b + 1), T), T)
            s_all[a, at, :] = scores
            g_all[a, at, :] = dot_nt(mvc[b], o_rows)
            return jnp.maximum(peak8, jnp.max(fold8(scores), 0))

        peak = jnp.max(lax.fori_loop(0, blocks[a], score, peaks[a]), 0, keepdims=True)

        def lift(n, state, a=a, peak=peak):
            mass8, weighted8 = state
            at = pl.ds(pl.multiple_of(n * 64, 64), 64)
            lifted = jnp.exp((s_all[a, at, :] - peak) * scale)
            s_all[a, at, :] = lifted
            mass8 = mass8 + jnp.sum(fold8(lifted), 0)
            weighted8 = weighted8 + jnp.sum(fold8(lifted * g_all[a, at, :]), 0)
            return mass8, weighted8

        none = jnp.zeros((8, T), F32)
        steps = (blocks[a] + 1) * (T // 64)
        mass8, weighted8 = lax.fori_loop(0, steps, lift, (none, none))
        inverse_mass = 1.0 / jnp.sum(mass8, 0, keepdims=True)
        row_delta = jnp.sum(weighted8, 0, keepdims=True) * inverse_mass

        def settle(n, state, a=a, inverse_mass=inverse_mass, row_delta=row_delta):
            at = pl.ds(pl.multiple_of(n * 64, 64), 64)
            attend = s_all[a, at, :] * inverse_mass
            p_all[a, at, :] = attend.astype(BF16)
            d_all[a, at, :] = (attend * (g_all[a, at, :] - row_delta)).astype(BF16)
            return state

        lax.fori_loop(0, steps, settle, 0)

    dmem_parts = []
    dmem_whole = []
    for b in range(N - 1, -1, -1):
        at = slice(T * (b + 1), T * (b + 2))
        for a in range(N - 1, -1, -1):
            rows = slice(a * T, (a + 1) * T)

            @pl.when(b < blocks[a])
            def _(a=a, rows=rows, at=at):
                add_k = dot_nn(d_all[a, at, :], qn[rows, :])
                add_v = dot_nn(p_all[a, at, :], ho[rows, :])
                if a < N - 1:
                    add_k = add_k + acc_k[...]
                    add_v = add_v + acc_v[...]
                acc_k[...] = add_k
                acc_v[...] = add_v

        @pl.when(b < blocks[N - 1])
        def _(b=b):
            sbk[b] = (acc_k[...] * scale).astype(BF16).reshape(N, M, HD)
            sbv[b] = acc_v[...].astype(BF16).reshape(N, M, HD)

        for n, (sb, rb) in enumerate(((sbk, rbk), (sbv, rbv))):
            for r in (1, 3, 2):
                to = lax.rem(j + r, N)
                copy = remote(
                    sb.at[b, to], rb.at[j, b], DMEM + 12 * n + 3 * b + r - 1, odev(r)
                )
                start_if(first_core, copy)
                dmem_parts.append((n, r, copy))
            whole = remote(
                sb.at[b], rb.at[j], DMEM1 + 4 * n + b, {"seq": place(c, i, b)}, DMEM1 + 4 * n + j
            )
            start_if((c == 1) & (b < j), whole)

    gain_q_sum = jnp.zeros((8, HD), F32)
    for a in range(N):
        rows = slice(a * T, (a + 1) * T)
        q_rows = qn[rows, :]

        def gather_q(b, total, a=a):
            at = pl.ds(pl.multiple_of(T * (b + 1), T), T)
            return total + dot_tn(d_all[a, at, :], mkc[b])

        grad_q = lax.fori_loop(0, blocks[a], gather_q, dot_tn(d_all[a, 0:T, :], kn[rows, :]))
        grad_q = grad_q * scale
        dkl[rows, :] = dot_nn(d_all[a, 0:T, :], q_rows) * scale
        dvl[rows, :] = dot_nn(p_all[a, 0:T, :], ho[rows, :])
        q_full = hq[rows, :].astype(F32)
        inv = icq[rows, :]
        gain_q_sum = gain_q_sum + jnp.sum(fold8(grad_q * q_full * inv), 0)
        gained = grad_q * gain_q
        aq[a] = (gained * inv).astype(BF16)
        pd[a, 0:1, :] = row_sum(gained * q_full)

    def homeward(src, dst, base):
        dst[i] = src[i]
        return [
            start(remote(src.at[lax.rem(i + r, N)], dst.at[i], base + r - 1, gdev(r)))
            for r in (1, 3, 2)
        ]

    home = homeward(aq, aqh, DQ)

    for m in range(N):
        at = slice(m * M, (m + 1) * M)
        block = m + c * (j - m)
        part = j + c * (m - j)
        acc_k[at, :] = sbk[block, part].astype(F32)
        acc_v[at, :] = sbv[block, part].astype(F32)
    for r in (1, 3, 2):
        source = lax.rem(j + N - r, N)

        @pl.when(first_core)
        def _(r=r):
            for _, q, copy in dmem_parts:
                if q == r:
                    copy.wait_recv()

        later = (c == 1) & (source > j)

        @pl.when(later)
        def _(source=source):
            for n, rb in ((0, rbk), (1, rbv)):
                remote(
                    rb.at[source], rb.at[source], DMEM1, odev(1), DMEM1 + 4 * n + source
                ).wait_recv()

        @pl.when(first_core | later)
        def _(source=source):
            acc_k[...] = acc_k[...] + rbk[source].reshape(N * M, HD).astype(F32)
            acc_v[...] = acc_v[...] + rbv[source].reshape(N * M, HD).astype(F32)

    grad_mem_k = acc_k[...].astype(BF16)
    grad_mem_v = acc_v[...].astype(BF16)

    square_k = dot_tn(ku[...], grad_mem_k)
    square_v = dot_tn(vu[...], grad_mem_v)
    for p in range(N):
        pay[0, p, 0:HD, :] = square_k[p * HD : (p + 1) * HD].astype(BF16)
        pay[1, p, 0:HD, :] = square_v[p * HD : (p + 1) * HD].astype(BF16)
    for n in range(KS):
        at = pl.ds(n, N * M, stride=KS)
        cols = slice(n * HD, (n + 1) * HD)
        dkl[at, :] = dkl[at, :] + dot_nt(grad_mem_k, wk_ref[cols, :])
        dvl[at, :] = dvl[at, :] + dot_nt(grad_mem_v, wv_ref[cols, :])
    gain_k_sum = jnp.zeros((8, HD), F32)
    for a in range(N):
        rows = slice(a * T, (a + 1) * T)
        av[a] = dvl[rows, :].astype(BF16)
        grad_k = dkl[rows, :]
        k_full = hk[rows, :].astype(F32)
        inv = ick[rows, :]
        gain_k_sum = gain_k_sum + jnp.sum(fold8(grad_k * k_full * inv), 0)
        gained = grad_k * gain_k
        ak[a] = (gained * inv).astype(BF16)
        pd[a, 1:2, :] = row_sum(gained * k_full)
    tail = PIECE - HD
    tail_k = jnp.broadcast_to(jnp.sum(gain_k_sum, 0, keepdims=True), (tail, HD)).astype(BF16)
    tail_q = jnp.broadcast_to(jnp.sum(gain_q_sum, 0, keepdims=True), (tail, HD)).astype(BF16)
    for p in range(N):
        pay[0, p, HD:PIECE, :] = tail_k
        pay[1, p, HD:PIECE, :] = tail_q

    scatter = [
        start(remote(pay.at[1 - c, p], rsi.at[1, j], RSX + p, cross(p), RSX + j))
        for p in range(N)
    ]
    scatter += [
        start(remote(pay.at[c, lax.rem(j + r, N)], rsi.at[0, j], RS + r - 1, odev(r)))
        for r in (1, 3, 2)
    ]
    home_pd = homeward(pd, pdh, PD)
    home += homeward(av, avh, DV)
    home += homeward(ak, akh, DK)

    for p in range(N):
        remote(pay.at[0, p], rsi.at[1, p], RSX + p, cross(p), RSX + p).wait_recv()
    for copy in scatter[N:]:
        copy.wait_recv()
    total = pay[c, j].astype(F32)
    for r in (1, 2, 3):
        total = total + rsi[0, lax.rem(j + r, N)].astype(F32)
    for p in range(N):
        total = total + rsi[1, p].astype(F32)
    full[c, j, i] = total.astype(BF16)
    agg = [
        start(remote(full.at[c, j, i], full.at[c, j, i], AGG + r - 1, gdev(r))) for r in (1, 3, 2)
    ]

    for copy in home_pd:
        copy.wait_recv()
    total = pdh[0]
    for h in range(1, N):
        total = total + pdh[h]
    zs2[z] = total
    z2 = [start(remote(zs2.at[z], zs2.at[z], Z2 + r - 1, zdev(r))) for r in range(1, nz)]

    for copy in agg:
        copy.wait_recv()
    ago = [start(remote(full.at[c, j], full.at[c, j], AGO + r - 1, odev(r))) for r in (1, 3, 2)]
    c2 = [start(remote(full.at[c, j], full.at[c, j], C2, cdev))]

    for copy in z2:
        copy.wait_recv()
    total = zs2[0]
    for r in range(1, nz):
        total = total + zs2[r]
    inverse = lax.rsqrt(gs[i] * (1.0 / hh) + EPS)
    shift = inverse * inverse * inverse * total * (1.0 / hh)
    shift_q = as_column(shift[0:1])
    shift_k = as_column(shift[1:2])
    for copy in home:
        copy.wait_recv()
    for h in range(N):
        cols = slice(h * HD, (h + 1) * HD)
        dq_out[:, cols] = (aqh[h].astype(F32) - q_ref[:, cols].astype(F32) * shift_q).astype(BF16)
        dk_out[:, cols] = (akh[h].astype(F32) - k_ref[:, cols].astype(F32) * shift_k).astype(BF16)
        dv_out[:, cols] = avh[h]

    for n, r in enumerate((1, 3, 2)):
        ago[n].wait_recv()
        at = full.at[c, lax.rem(j + N - r, N)]
        c2.append(start(remote(at, at, C2 + n + 1, cdev)))
    for copy in c2:
        copy.wait_recv()
    full_out[...] = full[...]

    for cond, copy in sent:
        if cond is None:
            copy.wait_send()
        else:
            pl.when(cond)(copy.wait_send)


def finish(
    dq_ref, dk_ref, dv_ref, full_ref,
    dq_out, dk_out, dv_out, qg_out, kg_out, sk_out, sv_out,
    sk_buf, sv_buf, sems,
):
    copies = [
        pltpu.make_async_copy(src, dst, sems.at[n])
        for n, (src, dst) in enumerate(((dq_ref, dq_out), (dk_ref, dk_out), (dv_ref, dv_out)))
    ]
    for copy in copies:
        copy.start()
    for n, (core, buf, out) in enumerate(((0, sk_buf, sk_out), (1, sv_buf, sv_out))):
        for h in range(N):
            for p in range(N):
                buf[h, p * HD : (p + 1) * HD, :] = full_ref[core, p, h, 0:HD, :].astype(F32)
            copy = pltpu.make_async_copy(buf.at[h], out.at[h], sems.at[3 + N * n + h])
            copy.start()
            copies.append(copy)
    for h in range(N):
        kg_out[h] = full_ref[0, 0, h, HD:PIECE, :].astype(F32)[0:1]
        qg_out[h] = full_ref[1, 0, h, HD:PIECE, :].astype(F32)[0:1]
    for copy in copies:
        copy.wait()


def on_device(nz, q, k, v, query_gain, key_gain, key_squeeze, value_squeeze, o):
    width = N * HD
    bf = functools.partial(pltpu.VMEM, dtype=BF16)
    ff = functools.partial(pltpu.VMEM, dtype=F32)
    rows = N * T
    deep = (N + 1) * T
    scratch = [bf((T, width))] * 4 + [bf((KS * HD, HD))] * 2
    scratch += [bf((rows, HD))] * 4 + [bf((rows, HD))] * 2 + [ff((rows, HD))] * 2
    scratch += [ff((rows, HD)), bf((N * M, KS * HD)), bf((N * M, KS * HD))]
    scratch += [ff((nz, 2, T)), ff((N, 2, T))]
    scratch += [bf((N, N, M, HD))] * 2 + [bf((N, N * M, HD))] * 2
    scratch += [ff((N, deep, T))] * 2 + [bf((N, deep, T))] * 2
    scratch += [ff((N * M, HD))] * 2 + [bf((N, N, M, HD))] * 4
    scratch += [ff((rows, HD))] * 2 + [bf((N, T, HD))] * 3 + [ff((N, 2, T))]
    scratch += [bf((N, T, HD))] * 3 + [ff((N, 2, T)), ff((nz, 2, T))]
    scratch += [bf((2, N, PIECE, HD))] * 2 + [bf((2, N, N, PIECE, HD))]
    scratch += [
        pltpu.SemaphoreType.DMA((N_SEM,)),
        pltpu.SemaphoreType.DMA((N_SEM,)),
        pltpu.SemaphoreType.DMA((10,)),
    ]
    vmem = pl.BlockSpec(memory_space=pltpu.VMEM)
    hbm = pl.BlockSpec(memory_space=pltpu.MemorySpace.HBM)
    stay = functools.partial(
        pltpu.with_memory_space_constraint, memory_space=pltpu.MemorySpace.HBM
    )
    grads = [jax.ShapeDtypeStruct((T, width), BF16)] * 3
    outs = pl.pallas_call(
        functools.partial(kernel, nz),
        out_shape=grads + [jax.ShapeDtypeStruct((2, N, N, PIECE, HD), BF16)],
        in_specs=[hbm] * 4 + [vmem] * 2 + [hbm] * 2,
        out_specs=[vmem] * 4,
        scratch_shapes=scratch,
        compiler_params=pltpu.CompilerParams(
            collective_id=0, has_side_effects=True, vmem_limit_bytes=40 * 2**20
        ),
    )(
        stay(q[0]), stay(k[0]), stay(v[0]), stay(o[0]),
        stay(query_gain.reshape(N, 1, HD)), stay(key_gain.reshape(N, 1, HD)),
        stay(key_squeeze), stay(value_squeeze),
    )
    kernels = jax.ShapeDtypeStruct((N, KS * HD, HD), F32)
    gains = jax.ShapeDtypeStruct((N, 1, HD), F32)
    dq, dk, dv, qg, kg, sk, sv = pl.pallas_call(
        finish,
        out_shape=grads + [gains] * 2 + [kernels] * 2,
        in_specs=[vmem] * 4,
        out_specs=[hbm] * 3 + [vmem] * 2 + [hbm] * 2,
        scratch_shapes=[
            ff((N, KS * HD, HD)), ff((N, KS * HD, HD)), pltpu.SemaphoreType.DMA((3 + 2 * N,)),
        ],
        compiler_params=pltpu.CompilerParams(vmem_limit_bytes=16 * 2**20),
    )(*outs)
    return dq[None], dk[None], dv[None], qg.reshape(width), kg.reshape(width), sk, sv


def solution(mesh):
    by_token = P("dp", "seq", "head")
    by_head = P("head", None, None)
    return jax.shard_map(
        functools.partial(on_device, mesh.shape["head"]),
        mesh=mesh,
        in_specs=(by_token,) * 3 + (P("head"), P("head"), by_head, by_head, by_token),
        out_specs=(by_token,) * 3 + (P("head"), P("head"), by_head, by_head),
        check_vma=False,
    )
```

time: 73.4 us -> 64.1 us (0.87)
  local copies, waits for them, and re-layouts: 8.93 us -> 0 us
    unnamed x15 -> x0, local copies, waits for them, and re-layouts: 8.93 us -> none
    pallas_call x1 -> x2, Pallas kernels: 63.6 us -> 63.4 us  [the longest x1 61.1 us: on_device(): pl.pallas_call(functools.partial(kernel, nz), out_shape=grads + [jax.Shap...]
where the time goes in v2:
time: 64.1 us; the launch traced here: 64 us
  Pallas kernels  63.4 us (99%)
    pallas_call x1, Pallas kernels, on_device(): pl.pallas_call(functools.partial(kernel, nz), out_shape=grads + [jax.Shap...  61.1 us
    pallas_call x1, Pallas kernels, on_device(): pl.pallas_call(finish, out_shape=grads + [gains] * 2 + [kernels] * 2, in_...  2.24 us

profile of v2, /device:TPU:1, one launch (start us, length us, event | category | flops | bytes accessed | tf_op | source)
XLA Modules:
  0.0 64.0 jit_solution(1471978695729741745)
XLA Ops:
  0.6 61.1 %shard_map.135 = (bf16[256,512]{1,0:T(8,128)(2,1)S(1)}, bf16[256,512]{1,0:T(8,128)(2,1)S(1)}, bf16[256,512]{1,0:T(8,128)(2,1)S(1)}, bf16[2,4,4,144,128]{4,3,2,1,0:T(8,128)(2,1)S(1)}) custom-call(bf16[256,512]{1,0:T(8,128)(2,1)} %bitcast.11, bf16[256,512]{1,0:T(8,128)(2,1)} %bitcast.12, bf16[256,512]{1,0:T(8,128)(2,1)} %bitcast.13, ...), custom_call_target="tpu_custom_call" | custom-call | tf_op jit(solution)/shard_map/pallas_call | solution.py:540
  61.8 2.2 %shard_map.136 = (bf16[256,512]{1,0:T(8,128)(2,1)}, bf16[256,512]{1,0:T(8,128)(2,1)}, bf16[256,512]{1,0:T(8,128)(2,1)}, f32[4,1,128]{2,1,0:T(1,128)}, f32[4,1,12...) custom-call(bf16[256,512]{1,0:T(8,128)(2,1)S(1)} %get-tuple-element.18.dq_ref, ...), custom_call_target="tpu_custom_call" | custom-call | tf_op jit(solution)/shard_map/pallas_call | solution.py:556

commit v3 on v2

--- a/solution.py
+++ b/solution.py
@@ -14,10 +14,10 @@
 M = 64
 EPS = 1e-06
 NEG = -1e30
+LOG2E = 1.4426950408889634
 MESH = pl.DeviceIdType.MESH
 F32 = jnp.float32
 BF16 = jnp.bfloat16
-PIECE = 144
 
 A2A = 0
 Z1 = A2A + 12
@@ -34,8 +34,12 @@
 RSX = RS + 3
 AGG = RSX + 4
 AGO = AGG + 3
-C2 = AGO + 3
-N_SEM = C2 + 4
+C2 = AGO + 12
+GM = C2 + 16
+GR = GM + 6
+GRX = GR + 3
+GG = GRX + 4
+N_SEM = GG + 3
 
 
 def dot_nt(a, b):
@@ -65,11 +69,12 @@
 def kernel(
     nz,
     q_hbm, k_hbm, v_hbm, o_hbm, gq_ref, gk_ref, wk_hbm, wv_hbm,
-    dq_out, dk_out, dv_out, full_out,
+    dq_out, dk_out, dv_out, full_out, gain_out,
     q_ref, k_ref, v_ref, o_ref, wk_ref, wv_ref,
     hq, hk, hv, ho, qn, kn, icq, ick, fs, ku, vu, zs, gs, mkg, mvg, mkc, mvc,
-    s_all, g_all, d_all, p_all, acc_k, acc_v, sbk, sbv, rbk, rbv,
-    dkl, dvl, aq, ak, av, pd, aqh, akh, avh, pdh, zs2,
+    p_all, g_all, m_all, fin, mkt, knt, dqt, acc_k, acc_v, sbk, sbv, rbk, rbv,
+    aq, ak, av, pd, aqh, akh, avh, pdh, zs2,
+    gmk, gmv, gmkh, gmvh, bkf, bvf, gmine, gsame, gother, gall,
     pay, rsi, full,
     ss, rs, loc,
 ):
@@ -134,7 +139,7 @@
         for n, (src, dst) in enumerate(
             (
                 (q_hbm, q_ref), (k_hbm, k_ref), (v_hbm, v_ref), (o_hbm, o_ref),
-                (wv_hbm.at[i], wv_ref), (wk_hbm.at[i], wk_ref),
+                (wv_hbm, wv_ref), (wk_hbm, wk_ref),
             )
         )
     ]
@@ -149,7 +154,7 @@
         for h in range(1, N):
             folded = folded + squares[:, h * HD : (h + 1) * HD]
         zs[z, row : row + 1, :] = row_sum(folded)
-    for copy in loads[2:]:
+    for copy in loads[2:4]:
         copy.wait()
 
     pl.semaphore_wait(barrier, len(peers))
@@ -188,6 +193,8 @@
     gs[i] = total
     g1 = [start(remote(gs.at[i], gs.at[i], G1 + r - 1, gdev(r))) for r in (1, 3, 2)]
     exchange(3, o_ref, ho)
+    for copy in loads[4:]:
+        copy.wait()
 
     def unfold(dst):
         for n in range(KS):
@@ -206,7 +213,7 @@
     arrived(0)
     fs[...] = hv[...].astype(F32)
     unfold(vu)
-    spread(mvg, dot_nn(vu[...], wv_ref[...]), 1)
+    spread(mvg, dot_nn(vu[...], wv_ref[i]), 1)
 
     for copy in g1:
         copy.wait_recv()
@@ -222,21 +229,34 @@
         kn[rows, :] = normed
         fs[rows, :] = normed.astype(F32)
     unfold(ku)
-    spread(mkg, dot_nn(ku[...], wk_ref[...]), 0)
+    spread(mkg, dot_nn(ku[...], wk_ref[i]), 0)
 
     arrived(2)
     arrived(3)
     key_at = lax.broadcasted_iota(jnp.int32, (T, T), 0)
     query_at = lax.broadcasted_iota(jnp.int32, (T, T), 1)
-    peaks = []
+    rate = scale * LOG2E
+
+    def score(a, block, mask, keys, values):
+        at = pl.ds(pl.multiple_of(block * T, T), T)
+        rows = slice(a * T, (a + 1) * T)
+        scores = jnp.where(mask, dot_nt(keys, qn[rows, :]), NEG)
+        grads = dot_nt(values, ho[rows, :])
+        peak = jnp.max(jnp.max(fold8(scores), 0), 0, keepdims=True)
+        lifted = jnp.exp2((scores - peak) * rate)
+        p_all[a, at, :] = lifted
+        g_all[a, at, :] = grads
+        m_all[a, block] = peak
+        mass = jnp.sum(jnp.sum(fold8(lifted), 0), 0, keepdims=True)
+        weighted = jnp.sum(jnp.sum(fold8(lifted * grads), 0), 0, keepdims=True)
+        return peak, mass, weighted
+
+    state = []
     for a in range(N):
         rows = slice(a * T, (a + 1) * T)
-        normed = (hq[rows, :].astype(F32) * icq[rows, :] * gain_q).astype(BF16)
-        qn[rows, :] = normed
-        scores = jnp.where(key_at <= query_at, dot_nt(kn[rows, :], normed), NEG)
-        s_all[a, 0:T, :] = scores
-        g_all[a, 0:T, :] = dot_nt(hv[rows, :], ho[rows, :])
-        peaks.append(jnp.max(fold8(scores), 0))
+        qn[rows, :] = (hq[rows, :].astype(F32) * icq[rows, :] * gain_q).astype(BF16)
+        state.append(score(a, 0, key_at <= query_at, kn[rows, :], hv[rows, :]))
+        knt[a] = jnp.transpose(kn[rows, :])
 
     for wanted, copy in mem_copies:
         pl.when(wanted)(copy.wait_recv)
@@ -247,67 +267,85 @@
             member = b + c * (t - b)
             mkc[b, at, :] = mkg[source, member]
             mvc[b, at, :] = mvg[source, member]
-
-    blocks = [a + c * (j - a) + 1 for a in range(N)]
+        mkt[b] = jnp.transpose(mkc[b])
+
+    edges = [a + c * (j - a) for a in range(N)]
     cuts = [M * (j + c * (a - j)) for a in range(N)]
-
+    blocks = [edges[a] + jnp.where(cuts[a] > 0, 1, 0) for a in range(N)]
+
+    for a in range(N):
+
+        def absorb(b, current, a=a):
+            old_peak, old_mass, old_weighted = current
+            limit = jnp.where(b == edges[a], cuts[a], T)
+            peak, mass, weighted = score(a, b + 1, key_at < limit, mkc[b], mvc[b])
+            top = jnp.maximum(old_peak, peak)
+            old_factor = jnp.exp2((old_peak - top) * rate)
+            factor = jnp.exp2((peak - top) * rate)
+            return (
+                top,
+                old_mass * old_factor + mass * factor,
+                old_weighted * old_factor + weighted * factor,
+            )
+
+        peak, mass, weighted = lax.fori_loop(0, blocks[a], absorb, state[a])
+        inverse_mass = 1.0 / mass
+        fin[a, 0] = peak
+        fin[a, 1] = inverse_mass
+        fin[a, 2] = weighted * inverse_mass
+
+    def settle(a, block):
+        at = pl.ds(pl.multiple_of(block * T, T), T)
+        factor = jnp.exp2((m_all[a, block] - fin[a, 0]) * rate) * fin[a, 1]
+        attend = p_all[a, at, :] * factor
+        d_scores = attend * (g_all[a, at, :] - fin[a, 2])
+        return attend.astype(BF16), d_scores.astype(BF16)
+
+    def homeward(src, dst, base):
+        dst[i] = src[i]
+        return [
+            start(remote(src.at[lax.rem(i + r, N)], dst.at[i], base + r - 1, gdev(r)))
+            for r in (1, 3, 2)
+        ]
+
+    def norm_side(grad, raw, inv, gain):
+        raw_full = raw.astype(F32)
+        gained = grad * gain
+        total = jnp.sum(fold8(grad * raw_full * inv), 0)
+        return total, (gained * inv).astype(BF16), row_sum(gained * raw_full)
+
+    gain_k_sum = jnp.zeros((8, HD), F32)
     for a in range(N):
         rows = slice(a * T, (a + 1) * T)
-        q_rows = qn[rows, :]
-        o_rows = ho[rows, :]
-
-        def score(b, peak8, a=a, q_rows=q_rows, o_rows=o_rows):
-            limit = jnp.where(b == blocks[a] - 1, cuts[a], T)
-            scores = jnp.where(key_at < limit, dot_nt(mkc[b], q_rows), NEG)
-            at = pl.ds(pl.multiple_of(T * (b + 1), T), T)
-            s_all[a, at, :] = scores
-            g_all[a, at, :] = dot_nt(mvc[b], o_rows)
-            return jnp.maximum(peak8, jnp.max(fold8(scores), 0))
-
-        peak = jnp.max(lax.fori_loop(0, blocks[a], score, peaks[a]), 0, keepdims=True)
-
-        def lift(n, state, a=a, peak=peak):
-            mass8, weighted8 = state
-            at = pl.ds(pl.multiple_of(n * 64, 64), 64)
-            lifted = jnp.exp((s_all[a, at, :] - peak) * scale)
-            s_all[a, at, :] = lifted
-            mass8 = mass8 + jnp.sum(fold8(lifted), 0)
-            weighted8 = weighted8 + jnp.sum(fold8(lifted * g_all[a, at, :]), 0)
-            return mass8, weighted8
-
-        none = jnp.zeros((8, T), F32)
-        steps = (blocks[a] + 1) * (T // 64)
-        mass8, weighted8 = lax.fori_loop(0, steps, lift, (none, none))
-        inverse_mass = 1.0 / jnp.sum(mass8, 0, keepdims=True)
-        row_delta = jnp.sum(weighted8, 0, keepdims=True) * inverse_mass
-
-        def settle(n, state, a=a, inverse_mass=inverse_mass, row_delta=row_delta):
-            at = pl.ds(pl.multiple_of(n * 64, 64), 64)
-            attend = s_all[a, at, :] * inverse_mass
-            p_all[a, at, :] = attend.astype(BF16)
-            d_all[a, at, :] = (attend * (g_all[a, at, :] - row_delta)).astype(BF16)
-            return state
-
-        lax.fori_loop(0, steps, settle, 0)
+        attend, d_scores = settle(a, 0)
+        dqt[a] = dot_nn(knt[a], d_scores)
+        grad_k = dot_nn(d_scores, qn[rows, :]) * scale
+        av[a] = dot_nn(attend, ho[rows, :]).astype(BF16)
+        total, ak[a], pd[a, 1:2, :] = norm_side(grad_k, hk[rows, :], ick[rows, :], gain_k)
+        gain_k_sum = gain_k_sum + total
+    home = homeward(av, avh, DV)
+    home += homeward(ak, akh, DK)
 
     dmem_parts = []
     dmem_whole = []
-    for b in range(N - 1, -1, -1):
-        at = slice(T * (b + 1), T * (b + 2))
-        for a in range(N - 1, -1, -1):
-            rows = slice(a * T, (a + 1) * T)
-
-            @pl.when(b < blocks[a])
-            def _(a=a, rows=rows, at=at):
-                add_k = dot_nn(d_all[a, at, :], qn[rows, :])
-                add_v = dot_nn(p_all[a, at, :], ho[rows, :])
-                if a < N - 1:
-                    add_k = add_k + acc_k[...]
-                    add_v = add_v + acc_v[...]
-                acc_k[...] = add_k
-                acc_v[...] = add_v
-
-        @pl.when(b < blocks[N - 1])
+    for b in range(N):
+        acc_k[...] = jnp.zeros((T, HD), F32)
+        acc_v[...] = jnp.zeros((T, HD), F32)
+
+        def add_up(a, nothing, b=b):
+            rows = pl.ds(pl.multiple_of(a * T, T), T)
+            attend, d_scores = settle(a, b + 1)
+            acc_k[...] = acc_k[...] + dot_nn(d_scores, qn[rows, :])
+            acc_v[...] = acc_v[...] + dot_nn(attend, ho[rows, :])
+            dqt[a] = dqt[a] + dot_nn(mkt[b], d_scores)
+            return nothing
+
+        past = jnp.where(j > 0, 0, 1)
+        within = jnp.where(b == j, 1, 0)
+        lowest = (1 - c) * (b + past) + c * jnp.where(b <= j, within, N)
+        lax.fori_loop(lowest, N, add_up, 0)
+
+        @pl.when(first_core | (b <= j))
         def _(b=b):
             sbk[b] = (acc_k[...] * scale).astype(BF16).reshape(N, M, HD)
             sbv[b] = acc_v[...].astype(BF16).reshape(N, M, HD)
@@ -328,31 +366,11 @@
     gain_q_sum = jnp.zeros((8, HD), F32)
     for a in range(N):
         rows = slice(a * T, (a + 1) * T)
-        q_rows = qn[rows, :]
-
-        def gather_q(b, total, a=a):
-            at = pl.ds(pl.multiple_of(T * (b + 1), T), T)
-            return total + dot_tn(d_all[a, at, :], mkc[b])
-
-        grad_q = lax.fori_loop(0, blocks[a], gather_q, dot_tn(d_all[a, 0:T, :], kn[rows, :]))
-        grad_q = grad_q * scale
-        dkl[rows, :] = dot_nn(d_all[a, 0:T, :], q_rows) * scale
-        dvl[rows, :] = dot_nn(p_all[a, 0:T, :], ho[rows, :])
-        q_full = hq[rows, :].astype(F32)
-        inv = icq[rows, :]
-        gain_q_sum = gain_q_sum + jnp.sum(fold8(grad_q * q_full * inv), 0)
-        gained = grad_q * gain_q
-        aq[a] = (gained * inv).astype(BF16)
-        pd[a, 0:1, :] = row_sum(gained * q_full)
-
-    def homeward(src, dst, base):
-        dst[i] = src[i]
-        return [
-            start(remote(src.at[lax.rem(i + r, N)], dst.at[i], base + r - 1, gdev(r)))
-            for r in (1, 3, 2)
-        ]
-
-    home = homeward(aq, aqh, DQ)
+        grad_q = jnp.transpose(dqt[a]) * scale
+        total, aq[a], pd[a, 0:1, :] = norm_side(grad_q, hq[rows, :], icq[rows, :], gain_q)
+        gain_q_sum = gain_q_sum + total
+
+    home_pd = homeward(pd, pdh, PD)
 
     for m in range(N):
         at = slice(m * M, (m + 1) * M)
@@ -389,30 +407,10 @@
     square_k = dot_tn(ku[...], grad_mem_k)
     square_v = dot_tn(vu[...], grad_mem_v)
     for p in range(N):
-        pay[0, p, 0:HD, :] = square_k[p * HD : (p + 1) * HD].astype(BF16)
-        pay[1, p, 0:HD, :] = square_v[p * HD : (p + 1) * HD].astype(BF16)
-    for n in range(KS):
-        at = pl.ds(n, N * M, stride=KS)
-        cols = slice(n * HD, (n + 1) * HD)
-        dkl[at, :] = dkl[at, :] + dot_nt(grad_mem_k, wk_ref[cols, :])
-        dvl[at, :] = dvl[at, :] + dot_nt(grad_mem_v, wv_ref[cols, :])
-    gain_k_sum = jnp.zeros((8, HD), F32)
-    for a in range(N):
-        rows = slice(a * T, (a + 1) * T)
-        av[a] = dvl[rows, :].astype(BF16)
-        grad_k = dkl[rows, :]
-        k_full = hk[rows, :].astype(F32)
-        inv = ick[rows, :]
-        gain_k_sum = gain_k_sum + jnp.sum(fold8(grad_k * k_full * inv), 0)
-        gained = grad_k * gain_k
-        ak[a] = (gained * inv).astype(BF16)
-        pd[a, 1:2, :] = row_sum(gained * k_full)
-    tail = PIECE - HD
-    tail_k = jnp.broadcast_to(jnp.sum(gain_k_sum, 0, keepdims=True), (tail, HD)).astype(BF16)
-    tail_q = jnp.broadcast_to(jnp.sum(gain_q_sum, 0, keepdims=True), (tail, HD)).astype(BF16)
-    for p in range(N):
-        pay[0, p, HD:PIECE, :] = tail_k
-        pay[1, p, HD:PIECE, :] = tail_q
+        pay[0, p] = square_k[p * HD : (p + 1) * HD].astype(BF16)
+        pay[1, p] = square_v[p * HD : (p + 1) * HD].astype(BF16)
+    gmk[...] = grad_mem_k.reshape(N, M, HD)
+    gmv[...] = grad_mem_v.reshape(N, M, HD)
 
     scatter = [
         start(remote(pay.at[1 - c, p], rsi.at[1, j], RSX + p, cross(p), RSX + j))
@@ -422,9 +420,43 @@
         start(remote(pay.at[c, lax.rem(j + r, N)], rsi.at[0, j], RS + r - 1, odev(r)))
         for r in (1, 3, 2)
     ]
-    home_pd = homeward(pd, pdh, PD)
-    home += homeward(av, avh, DV)
-    home += homeward(ak, akh, DK)
+    slots = homeward(gmk, gmkh, GM) + homeward(gmv, gmvh, GM + 3)
+
+    crossed = square_k[0:HD] * wk_ref[i, 0:HD, :].astype(F32)
+    for p in range(1, N):
+        at = slice(p * HD, (p + 1) * HD)
+        crossed = crossed + square_k[at] * wk_ref[i, at, :].astype(F32)
+    gmine[0:1, :] = jnp.sum(gain_q_sum, 0, keepdims=True)
+    gmine[1:2, :] = jnp.sum(gain_k_sum, 0, keepdims=True) + row_sum(crossed) / gain_k
+    gains = [start(remote(gmine, gsame.at[j], GR + r - 1, odev(r))) for r in (1, 3, 2)]
+    for p in range(N):
+        start(remote(gmine, gother.at[j], GRX + p, cross(p), GRX + j))
+
+    home += homeward(aq, aqh, DQ)
+
+    for copy in slots:
+        copy.wait_recv()
+    product = jnp.zeros((T, HD), F32)
+    for h in range(N):
+        spread_k = dot_nt(gmkh[h], wk_ref[h])
+        spread_v = dot_nt(gmvh[h], wv_ref[h])
+        for n in range(KS):
+            at = pl.ds(n, M, stride=KS)
+            cols = slice(n * HD, (n + 1) * HD)
+            bkf[h, at, :] = spread_k[:, cols]
+            bvf[h, at, :] = spread_v[:, cols]
+        gained = bkf[h] * gk_ref[h]
+        bkf[h] = gained
+        product = product + gained * k_ref[:, h * HD : (h + 1) * HD].astype(F32)
+
+    for copy in home_pd:
+        copy.wait_recv()
+    total = pdh[0]
+    for h in range(1, N):
+        total = total + pdh[h]
+    zs2[z, 0:1, :] = total[0:1]
+    zs2[z, 1:2, :] = total[1:2] + row_sum(product)
+    z2 = [start(remote(zs2.at[z], zs2.at[z], Z2 + r - 1, zdev(r))) for r in range(1, nz)]
 
     for p in range(N):
         remote(pay.at[0, p], rsi.at[1, p], RSX + p, cross(p), RSX + p).wait_recv()
@@ -439,19 +471,32 @@
     agg = [
         start(remote(full.at[c, j, i], full.at[c, j, i], AGG + r - 1, gdev(r))) for r in (1, 3, 2)
     ]
-
-    for copy in home_pd:
-        copy.wait_recv()
-    total = pdh[0]
-    for h in range(1, N):
-        total = total + pdh[h]
-    zs2[z] = total
-    z2 = [start(remote(zs2.at[z], zs2.at[z], Z2 + r - 1, zdev(r))) for r in range(1, nz)]
-
-    for copy in agg:
-        copy.wait_recv()
-    ago = [start(remote(full.at[c, j], full.at[c, j], AGO + r - 1, odev(r))) for r in (1, 3, 2)]
-    c2 = [start(remote(full.at[c, j], full.at[c, j], C2, cdev))]
+    ago = {}
+    c2 = []
+
+    def pass_on(slot, member):
+        piece = full.at[c, j, member]
+        for r in (1, 3, 2):
+            ago[r, slot] = start(remote(piece, piece, AGO + 4 * (r - 1) + slot, odev(r)))
+        c2.append(start(remote(piece, piece, C2 + slot, cdev)))
+
+    pass_on(0, i)
+
+    for copy in gains:
+        copy.wait_recv()
+    for p in range(N):
+        remote(gmine, gother.at[p], GRX + p, cross(p), GRX + p).wait_recv()
+    total = gmine[...]
+    for r in (1, 2, 3):
+        total = total + gsame[lax.rem(j + r, N)]
+    for p in range(N):
+        total = total + gother[p]
+    gall[i] = total
+    gg = [start(remote(gall.at[i], gall.at[i], GG + r - 1, gdev(r))) for r in (1, 3, 2)]
+
+    for n, r in enumerate((1, 3, 2)):
+        agg[n].wait_recv()
+        pass_on(n + 1, lax.rem(i + N - r, N))
 
     for copy in z2:
         copy.wait_recv()
@@ -464,16 +509,22 @@
     shift_k = as_column(shift[1:2])
     for copy in home:
         copy.wait_recv()
+    inverse_k = as_column(inverse[1:2])
     for h in range(N):
         cols = slice(h * HD, (h + 1) * HD)
         dq_out[:, cols] = (aqh[h].astype(F32) - q_ref[:, cols].astype(F32) * shift_q).astype(BF16)
-        dk_out[:, cols] = (akh[h].astype(F32) - k_ref[:, cols].astype(F32) * shift_k).astype(BF16)
-        dv_out[:, cols] = avh[h]
-
-    for n, r in enumerate((1, 3, 2)):
-        ago[n].wait_recv()
-        at = full.at[c, lax.rem(j + N - r, N)]
-        c2.append(start(remote(at, at, C2 + n + 1, cdev)))
+        grad_k = akh[h].astype(F32) + bkf[h] * inverse_k
+        dk_out[:, cols] = (grad_k - k_ref[:, cols].astype(F32) * shift_k).astype(BF16)
+        dv_out[:, cols] = (avh[h].astype(F32) + bvf[h]).astype(BF16)
+    for copy in gg:
+        copy.wait_recv()
+    gain_out[...] = gall[...]
+
+    for slot, back in enumerate((0, 1, 3, 2)):
+        for n, r in enumerate((1, 3, 2)):
+            ago[r, slot].wait_recv()
+            at = full.at[c, lax.rem(j + N - r, N), lax.rem(i + N - back, N)]
+            c2.append(start(remote(at, at, C2 + 4 + 3 * slot + n, cdev)))
     for copy in c2:
         copy.wait_recv()
     full_out[...] = full[...]
@@ -486,7 +537,7 @@
 
 
 def finish(
-    dq_ref, dk_ref, dv_ref, full_ref,
+    dq_ref, dk_ref, dv_ref, full_ref, gain_ref,
     dq_out, dk_out, dv_out, qg_out, kg_out, sk_out, sv_out,
     sk_buf, sv_buf, sems,
 ):
@@ -504,8 +555,8 @@
             copy.start()
             copies.append(copy)
     for h in range(N):
-        kg_out[h] = full_ref[0, 0, h, HD:PIECE, :].astype(F32)[0:1]
-        qg_out[h] = full_ref[1, 0, h, HD:PIECE, :].astype(F32)[0:1]
+        qg_out[h] = gain_ref[h, 0:1, :]
+        kg_out[h] = gain_ref[h, 1:2, :]
     for copy in copies:
         copy.wait()
 
@@ -516,16 +567,19 @@
     ff = functools.partial(pltpu.VMEM, dtype=F32)
     rows = N * T
     deep = (N + 1) * T
-    scratch = [bf((T, width))] * 4 + [bf((KS * HD, HD))] * 2
+    scratch = [bf((T, width))] * 4 + [bf((N, KS * HD, HD))] * 2
     scratch += [bf((rows, HD))] * 4 + [bf((rows, HD))] * 2 + [ff((rows, HD))] * 2
     scratch += [ff((rows, HD)), bf((N * M, KS * HD)), bf((N * M, KS * HD))]
     scratch += [ff((nz, 2, T)), ff((N, 2, T))]
     scratch += [bf((N, N, M, HD))] * 2 + [bf((N, N * M, HD))] * 2
-    scratch += [ff((N, deep, T))] * 2 + [bf((N, deep, T))] * 2
+    scratch += [ff((N, deep, T))] * 2 + [ff((N, N + 1, 1, T)), ff((N, 3, 1, T))]
+    scratch += [bf((N, HD, T))] * 2 + [ff((N, HD, T))]
     scratch += [ff((N * M, HD))] * 2 + [bf((N, N, M, HD))] * 4
-    scratch += [ff((rows, HD))] * 2 + [bf((N, T, HD))] * 3 + [ff((N, 2, T))]
+    scratch += [bf((N, T, HD))] * 3 + [ff((N, 2, T))]
     scratch += [bf((N, T, HD))] * 3 + [ff((N, 2, T)), ff((nz, 2, T))]
-    scratch += [bf((2, N, PIECE, HD))] * 2 + [bf((2, N, N, PIECE, HD))]
+    scratch += [bf((N, M, HD))] * 4 + [ff((N, T, HD))] * 2
+    scratch += [ff((2, HD))] + [ff((N, 2, HD))] * 3
+    scratch += [bf((2, N, HD, HD))] * 2 + [bf((2, N, N, HD, HD))]
     scratch += [
         pltpu.SemaphoreType.DMA((N_SEM,)),
         pltpu.SemaphoreType.DMA((N_SEM,)),
@@ -539,9 +593,10 @@
     grads = [jax.ShapeDtypeStruct((T, width), BF16)] * 3
     outs = pl.pallas_call(
         functools.partial(kernel, nz),
-        out_shape=grads + [jax.ShapeDtypeStruct((2, N, N, PIECE, HD), BF16)],
+        out_shape=grads
+        + [jax.ShapeDtypeStruct((2, N, N, HD, HD), BF16), jax.ShapeDtypeStruct((N, 2, HD), F32)],
         in_specs=[hbm] * 4 + [vmem] * 2 + [hbm] * 2,
-        out_specs=[vmem] * 4,
+        out_specs=[vmem] * 5,
         scratch_shapes=scratch,
         compiler_params=pltpu.CompilerParams(
             collective_id=0, has_side_effects=True, vmem_limit_bytes=40 * 2**20
@@ -556,7 +611,7 @@
     dq, dk, dv, qg, kg, sk, sv = pl.pallas_call(
         finish,
         out_shape=grads + [gains] * 2 + [kernels] * 2,
-        in_specs=[vmem] * 4,
+        in_specs=[vmem] * 5,
         out_specs=[hbm] * 3 + [vmem] * 2 + [hbm] * 2,
         scratch_shapes=[
             ff((N, KS * HD, HD)), ff((N, KS * HD, HD)), pltpu.SemaphoreType.DMA((3 + 2 * N,)),

time: 64.1 us -> 59.9 us (0.934)
  Pallas kernels: 63.4 us -> 59.1 us
    pallas_call x1, Pallas kernels: 61.1 us -> 56.9 us  [on_device(): pl.pallas_call(functools.partial(kernel, nz), out_shape=grads + [jax.Shap...]
where the time goes in v3:
time: 59.9 us; the launch traced here: 59.8 us
  Pallas kernels  59.1 us (99%)
  between operations  0.64 us (1%)
    pallas_call x1, Pallas kernels, on_device(): pl.pallas_call(functools.partial(kernel, nz), out_shape=grads + [jax.Shap...  56.9 us
    pallas_call x1, Pallas kernels, on_device(): pl.pallas_call(finish, out_shape=grads + [gains] * 2 + [kernels] * 2, in_...  2.24 us

profile of v3, /device:TPU:1, one launch (start us, length us, event | category | flops | bytes accessed | tf_op | source)
XLA Modules:
  0.0 59.8 jit_solution(13041768252397598940)
XLA Ops:
  0.6 56.9 %shard_map.135 = (bf16[256,512]{1,0:T(8,128)(2,1)S(1)}, bf16[256,512]{1,0:T(8,128)(2,1)S(1)}, bf16[256,512]{1,0:T(8,128)(2,1)S(1)}, bf16[2,4,4,128,128]{4,3,2,1,0:T(8,128)(2,1)S(1)}, f32[4,2,128]{2,1,0:T(2,128)S(1)}) custom-call(bf16[256,512]{1,0:T(8,128)(2,1)} %bitcast.11, bf16[256,512]{1,0:T(8,128)(2,1)} %bitcast.12, bf16[256,512]{1,0:T(8,128)(2,1)} %bitcast.13, ...), custom_call_target="tpu_custom_call" | custom-call | tf_op jit(solution)/shard_map/pallas_call | solution.py:594
  57.5 2.2 %shard_map.136 = (bf16[256,512]{1,0:T(8,128)(2,1)}, bf16[256,512]{1,0:T(8,128)(2,1)}, bf16[256,512]{1,0:T(8,128)(2,1)}, f32[4,1,128]{2,1,0:T(1,128)}, f32[4,1,12...) custom-call(bf16[256,512]{1,0:T(8,128)(2,1)S(1)} %get-tuple-element.19.dq_ref, ...), custom_call_target="tpu_custom_call" | custom-call | tf_op jit(solution)/shard_map/pallas_call | solution.py:611

commit v4 on v3

v4 whole, which is shorter than its diff:
```python
import functools

import jax
import jax.numpy as jnp
from jax import lax
from jax.experimental import pallas as pl
from jax.experimental.pallas import tpu as pltpu
from jax.sharding import PartitionSpec as P

HD = 128
KS = 4
N = 4
T = 256
M = 64
EPS = 1e-06
NEG = -1e30
LOG2E = 1.4426950408889634
MESH = pl.DeviceIdType.MESH
F32 = jnp.float32
BF16 = jnp.bfloat16

A2A = 0
Z1 = A2A + 4
G1 = Z1 + 1
MEM = G1 + 1
DMEM = MEM + 2
DMEM3 = DMEM + 2
DQ = DMEM3 + 6
DK = DQ + 1
DV = DK + 1
PD = DV + 1
Z2 = PD + 1
RS = Z2 + 1
RSX = RS + 1
AGG = RSX + 1
AGO = AGG + 3
C2 = AGO + 4
GM = C2 + 8
GR = GM + 2
GRX = GR + 1
GG = GRX + 1
N_RECV = GG + 1
N_SEND = 4 + 6


def dot_nt(a, b):
    return lax.dot_general(a, b, (((1,), (1,)), ((), ())), preferred_element_type=F32)


def dot_tn(a, b):
    return lax.dot_general(a, b, (((0,), (0,)), ((), ())), preferred_element_type=F32)


def dot_nn(a, b):
    return lax.dot_general(a, b, (((1,), (0,)), ((), ())), preferred_element_type=F32)


def as_column(row):
    return jnp.transpose(jnp.broadcast_to(row, (HD, row.shape[1])))


def row_sum(block):
    return jnp.sum(jnp.transpose(block), 0, keepdims=True)


def fold8(block):
    return block.reshape(block.shape[0] // 8, 8, block.shape[1])


def kernel(
    nz,
    q_hbm, k_hbm, v_hbm, o_hbm, gq_hbm, gk_hbm, wk_hbm, wv_hbm,
    dq_out, dk_out, dv_out, kern_out, gain_out,
    gq_ref, gk_ref, dq_buf, dk_buf, dv_buf, kern, gain_buf, q_ref, k_ref, v_ref, o_ref, wk_ref, wv_ref,
    hq, hk, hv, ho, qn, kn, icq, ick, fs, ku, vu, gsp, zs, gs, mkg, mvg, mkc, mvc,
    p_all, g_all, m_all, fin, mkt, knt, dqt, acc_k, acc_v, sbk, sbv, rbk, rbv,
    aq, ak, av, pd, aqh, akh, avh, pdh, zs2,
    gmk, gmv, gmkh, gmvh, bkf, bvf, gmine, gsame, gother, gall,
    pay, rsi, full, tally,
    ss, rs, loc, out_sem,
):
    seq = lax.axis_index("seq")
    x = lax.rem(seq, N)
    y = lax.div(seq, N)
    z = lax.axis_index("head")
    c = lax.axis_index("dp")
    i = y
    j = x
    near = i + c * (j - i)
    far = j + c * (i - j)
    hh = nz * N * HD
    scale = HD ** (-0.5)

    def gdev(r):
        return {"seq": lax.rem(i + r, N) * N + j}

    def odev(r):
        return {"seq": i * N + lax.rem(j + r, N)}

    def ndev(r):
        to = lax.rem(near + r, N)
        return {"seq": to * (N - (N - 1) * c) + far * (1 + (N - 1) * c)}

    def fdev(r):
        to = lax.rem(far + r, N)
        return {"seq": near * (N - (N - 1) * c) + to * (1 + (N - 1) * c)}

    def cross(p):
        return {"seq": i * N + p, "dp": 1 - c}

    def zdev(r):
        return {"head": lax.rem(z + r, nz)}

    cdev = {"dp": 1 - c}

    def remote(src, dst, index, device, group):
        return pltpu.make_async_remote_copy(
            src_ref=src,
            dst_ref=dst,
            send_sem=ss.at[group],
            recv_sem=rs.at[index],
            device_id=device,
            device_id_type=MESH,
        )

    sent = [0, 0, 0, 0]

    def send(src, dst, index, device, group):
        remote(src, dst, index, device, group).start()
        size = 1
        for length in src.shape:
            size = size * length
        sent[group] += size * src.dtype.itemsize

    def landed(index, space):
        remote(space, space, index, cdev, 0).wait_recv()

    written = []

    def write(src, dst, index):
        copy = pltpu.make_async_copy(src, dst, out_sem.at[index])
        copy.start()
        written.append(copy)

    def emit(core, across, along):
        head = along + core * (across - along)
        rows = pl.ds(pl.multiple_of((across + core * (along - across)) * HD, HD), HD)
        kern[core, head, rows, :] = full[core, across, along].astype(F32)
        copy = pltpu.make_async_copy(
            kern.at[core, head, rows, :], kern_out.at[core, head, rows, :], out_sem.at[0]
        )
        copy.start()


    barrier = pltpu.get_barrier_semaphore()
    peers = [gdev(r) for r in (1, 2, 3)] + [odev(r) for r in (1, 2, 3)]
    peers += [zdev(r) for r in range(1, nz)] + [cross(p) for p in range(N)] + [cdev]
    for peer in peers:
        pl.semaphore_signal(barrier, inc=1, device_id=peer, device_id_type=MESH)

    loads = [
        pltpu.make_async_copy(src, dst, loc.at[4 + n])
        for n, (src, dst) in enumerate(
            (
                (q_hbm, q_ref), (k_hbm, k_ref), (v_hbm, v_ref), (o_hbm, o_ref),
                (wv_hbm, wv_ref), (wk_hbm, wk_ref),
                (gq_hbm, gq_ref), (gk_hbm, gk_ref),
            )
        )
    ]
    for copy in loads:
        copy.start()

    for row, ref in ((0, q_ref), (1, k_ref)):
        loads[row].wait()
        full_rows = ref[...].astype(F32)
        squares = full_rows * full_rows
        folded = squares[:, :HD]
        for h in range(1, N):
            folded = folded + squares[:, h * HD : (h + 1) * HD]
        gsp[i, row : row + 1, :] = row_sum(folded)
    for copy in loads[2:4]:
        copy.wait()

    pl.semaphore_wait(barrier, len(peers))

    for r in (2, 1, 3):
        send(gsp.at[i], gsp.at[i], G1, gdev(r), 3)
    rows_mine = pl.ds(pl.multiple_of(i * T, T), T)
    own = {}

    def exchange(n, src, dst):
        for r in (1, 3, 2):
            cols = pl.ds(pl.multiple_of(lax.rem(i + r, N) * HD, HD), HD)
            send(src.at[:, cols], dst.at[rows_mine, :], A2A + n, gdev(r), 0)
        cols = pl.ds(pl.multiple_of(i * HD, HD), HD)
        own[n] = pltpu.make_async_copy(src.at[:, cols], dst.at[rows_mine, :], loc.at[n])
        own[n].start()

    def arrived(n):
        landed(A2A + n, hv.at[0 : 3 * T, :])
        own[n].wait()

    exchange(0, v_ref, hv)
    exchange(1, k_ref, hk)

    exchange(2, q_ref, hq)
    exchange(3, o_ref, ho)

    landed(G1, gsp.at[0:3])
    for r in range(1, nz):
        send(gsp, zs.at[z], Z1, zdev(r), 0)
    for copy in loads[4:]:
        copy.wait()

    def unfold(dst):
        for n in range(KS):
            dst[:, n * HD : (n + 1) * HD] = fs[pl.ds(n, N * M, stride=KS), :].astype(BF16)

    def spread(mem, value, index):
        mem[j] = value.astype(BF16).reshape(N, M, HD)
        for r in (1, 3, 2):
            send(mem.at[j], mem.at[j], MEM + index, odev(r), 0)

    arrived(0)
    fs[...] = hv[...].astype(F32)
    unfold(vu)
    spread(mvg, dot_nn(vu[...], wv_ref[i]), 1)

    landed(Z1, zs.at[0 : nz - 1])
    gs[...] = gsp[...]
    for r in range(1, nz):
        gs[...] = gs[...] + zs[lax.rem(z + r, nz)]
    gain_q = gq_ref[i]
    gain_k = gk_ref[i]
    arrived(1)
    for a in range(N):
        rows = slice(a * T, (a + 1) * T)
        inverse = lax.rsqrt(gs[a] * (1.0 / hh) + EPS)
        icq[rows, :] = as_column(inverse[0:1])
        ick[rows, :] = as_column(inverse[1:2])
        normed = (hk[rows, :].astype(F32) * ick[rows, :] * gain_k).astype(BF16)
        kn[rows, :] = normed
        fs[rows, :] = normed.astype(F32)
    unfold(ku)
    spread(mkg, dot_nn(ku[...], wk_ref[i]), 0)

    arrived(2)
    arrived(3)
    key_at = lax.broadcasted_iota(jnp.int32, (T, T), 0)
    query_at = lax.broadcasted_iota(jnp.int32, (T, T), 1)
    rate = scale * LOG2E

    def score(a, block, mask, keys, values):
        at = pl.ds(pl.multiple_of(block * T, T), T)
        rows = slice(a * T, (a + 1) * T)
        scores = jnp.where(mask, dot_nt(keys, qn[rows, :]), NEG)
        grads = dot_nt(values, ho[rows, :])
        peak = jnp.max(jnp.max(fold8(scores), 0), 0, keepdims=True)
        lifted = jnp.exp2((scores - peak) * rate)
        p_all[a, at, :] = lifted
        g_all[a, at, :] = grads
        m_all[a, block] = peak
        mass = jnp.sum(jnp.sum(fold8(lifted), 0), 0, keepdims=True)
        weighted = jnp.sum(jnp.sum(fold8(lifted * grads), 0), 0, keepdims=True)
        return peak, mass, weighted

    state = []
    for a in range(N):
        rows = slice(a * T, (a + 1) * T)
        qn[rows, :] = (hq[rows, :].astype(F32) * icq[rows, :] * gain_q).astype(BF16)
        state.append(score(a, 0, key_at <= query_at, kn[rows, :], hv[rows, :]))
        knt[a] = jnp.transpose(kn[rows, :])

    landed(MEM, mkg.at[0:3])
    landed(MEM + 1, mvg.at[0:3])
    for b in range(N):
        for t in range(N):
            at = slice(t * M, (t + 1) * M)
            mkc[b, at, :] = mkg[t, b]
            mvc[b, at, :] = mvg[t, b]
        mkt[b] = jnp.transpose(mkc[b])

    past = jnp.where(j > 0, 0, 1)

    for a in range(N):

        def absorb(b, current, a=a):
            old_peak, old_mass, old_weighted = current
            limit = jnp.where(b == a, j * M, T)
            peak, mass, weighted = score(a, b + 1, key_at < limit, mkc[b], mvc[b])
            top = jnp.maximum(old_peak, peak)
            old_factor = jnp.exp2((old_peak - top) * rate)
            factor = jnp.exp2((peak - top) * rate)
            return (
                top,
                old_mass * old_factor + mass * factor,
                old_weighted * old_factor + weighted * factor,
            )

        peak, mass, weighted = lax.fori_loop(0, a + 1 - past, absorb, state[a])
        inverse_mass = 1.0 / mass
        fin[a, 0] = peak
        fin[a, 1] = inverse_mass
        fin[a, 2] = weighted * inverse_mass

    def settle(a, block):
        at = pl.ds(pl.multiple_of(block * T, T), T)
        factor = jnp.exp2((m_all[a, block] - fin[a, 0]) * rate) * fin[a, 1]
        attend = p_all[a, at, :] * factor
        d_scores = attend * (g_all[a, at, :] - fin[a, 2])
        return attend.astype(BF16), d_scores.astype(BF16)

    def homeward(src, dst, index, group=1):
        dst[i] = src[i]
        for r in (1, 3, 2):
            send(src.at[lax.rem(i + r, N)], dst.at[i], index, gdev(r), group)

    def norm_side(grad, raw, inv, gain):
        raw_full = raw.astype(F32)
        gained = grad * gain
        total = jnp.sum(fold8(grad * raw_full * inv), 0)
        return total, (gained * inv).astype(BF16), row_sum(gained * raw_full)

    gain_k_sum = jnp.zeros((8, HD), F32)
    for a in range(N):
        rows = slice(a * T, (a + 1) * T)
        attend, d_scores = settle(a, 0)
        dqt[a] = dot_nn(knt[a], d_scores)
        grad_k = dot_nn(d_scores, qn[rows, :]) * scale
        av[a] = dot_nn(attend, ho[rows, :]).astype(BF16)
        total, ak[a], pd[a, 1:2, :] = norm_side(grad_k, hk[rows, :], ick[rows, :], gain_k)
        gain_k_sum = gain_k_sum + total
    homeward(av, avh, DV)
    homeward(ak, akh, DK)

    last_parts = []
    for b in range(N):
        acc_k[...] = jnp.zeros((T, HD), F32)
        acc_v[...] = jnp.zeros((T, HD), F32)

        def add_up(a, nothing, b=b):
            rows = pl.ds(pl.multiple_of(a * T, T), T)
            attend, d_scores = settle(a, b + 1)
            acc_k[...] = acc_k[...] + dot_nn(d_scores, qn[rows, :])
            acc_v[...] = acc_v[...] + dot_nn(attend, ho[rows, :])
            dqt[a] = dqt[a] + dot_nn(mkt[b], d_scores)
            return nothing

        lax.fori_loop(b + past, N, add_up, 0)

        sbk[b] = (acc_k[...] * scale).astype(BF16).reshape(N, M, HD)
        sbv[b] = acc_v[...].astype(BF16).reshape(N, M, HD)
        for n, (sb, rb) in enumerate(((sbk, rbk), (sbv, rbv))):
            for r in (2, 1, 3):
                to = lax.rem(j + r, N)
                if b < N - 1:
                    send(sb.at[b, to], rb.at[j, b], DMEM + n, odev(r), 1)
                else:
                    index = 3 * n + r - 1
                    copy = remote(sb.at[b, to], rb.at[j, b], DMEM3 + index, odev(r), 4 + index)
                    pl.when(to < j)(copy.start)
                    last_parts.append((to < j, copy))

    gain_q_sum = jnp.zeros((8, HD), F32)
    for a in range(N):
        rows = slice(a * T, (a + 1) * T)
        grad_q = jnp.transpose(dqt[a]) * scale
        total, aq[a], pd[a, 0:1, :] = norm_side(grad_q, hq[rows, :], icq[rows, :], gain_q)
        gain_q_sum = gain_q_sum + total

    homeward(pd, pdh, PD, 3)
    homeward(aq, aqh, DQ)

    for m in range(N):
        at = slice(m * M, (m + 1) * M)
        acc_k[at, :] = sbk[m, j].astype(F32)
        acc_v[at, :] = sbv[m, j].astype(F32)
    for n in range(2):
        landed(DMEM + n, hv.at[0 : 9 * M, :])
    for r in (1, 3, 2):
        source = lax.rem(j + N - r, N)
        for n, (rb, acc) in enumerate(((rbk, acc_k), (rbv, acc_v))):
            at = slice(0, (N - 1) * M)
            acc[at, :] = acc[at, :] + rb[source, 0 : N - 1].reshape((N - 1) * M, HD).astype(F32)

            @pl.when(source > j)
            def _(source=source, n=n, r=r, rb=rb, acc=acc):
                landed(DMEM3 + 3 * n + r - 1, rb.at[source, N - 1])
                at = slice((N - 1) * M, N * M)
                acc[at, :] = acc[at, :] + rb[source, N - 1].astype(F32)

    grad_mem_k = acc_k[...].astype(BF16)
    grad_mem_v = acc_v[...].astype(BF16)

    square_k = dot_tn(ku[...], grad_mem_k)
    square_v = dot_tn(vu[...], grad_mem_v)
    for p in range(N):
        pay[0, p] = square_k[p * HD : (p + 1) * HD].astype(BF16)
        pay[1, p] = square_v[p * HD : (p + 1) * HD].astype(BF16)
    gmk[...] = grad_mem_k.reshape(N, M, HD)
    gmv[...] = grad_mem_v.reshape(N, M, HD)

    for p in range(N):
        send(pay.at[1 - c, p], rsi.at[1, j], RSX, cross(p), 2)
    for r in (1, 3, 2):
        send(pay.at[c, lax.rem(j + r, N)], rsi.at[0, j], RS, odev(r), 2)
    homeward(gmk, gmkh, GM)
    homeward(gmv, gmvh, GM + 1)

    crossed = square_k[0:HD] * wk_ref[i, 0:HD, :].astype(F32)
    for p in range(1, N):
        at = slice(p * HD, (p + 1) * HD)
        crossed = crossed + square_k[at] * wk_ref[i, at, :].astype(F32)
    gmine[0:1, :] = jnp.sum(gain_q_sum, 0, keepdims=True)
    gmine[1:2, :] = jnp.sum(gain_k_sum, 0, keepdims=True) + row_sum(crossed) / gain_k
    for r in (1, 3, 2):
        send(gmine, gsame.at[j], GR, odev(r), 3)
    for p in range(N):
        send(gmine, gother.at[j], GRX, cross(p), 3)

    landed(GM, gmkh.at[0:3])
    landed(GM + 1, gmvh.at[0:3])
    product = jnp.zeros((T, HD), F32)
    for h in range(N):
        spread_k = dot_nt(gmkh[h], wk_ref[h])
        spread_v = dot_nt(gmvh[h], wv_ref[h])
        for n in range(KS):
            at = pl.ds(n, M, stride=KS)
            cols = slice(n * HD, (n + 1) * HD)
            bkf[h, at, :] = spread_k[:, cols]
            bvf[h, at, :] = spread_v[:, cols]
        gained = bkf[h] * gk_ref[h]
        bkf[h] = gained
        product = product + gained * k_ref[:, h * HD : (h + 1) * HD].astype(F32)

    landed(PD, pdh.at[0:3])
    total = pdh[0]
    for h in range(1, N):
        total = total + pdh[h]
    zs2[z, 0:1, :] = total[0:1]
    zs2[z, 1:2, :] = total[1:2] + row_sum(product)
    for r in range(1, nz):
        send(zs2.at[z], zs2.at[z], Z2, zdev(r), 3)

    landed(RSX, rsi.at[1])
    landed(RS, rsi.at[0, 0:3])
    total = pay[c, j].astype(F32)
    for r in (1, 2, 3):
        total = total + rsi[0, lax.rem(j + r, N)].astype(F32)
    for p in range(N):
        total = total + rsi[1, p].astype(F32)
    full[c, far, near] = total.astype(BF16)
    mine = full.at[c, far, near]
    for n, r in enumerate((1, 3, 2)):
        send(mine, mine, AGG + n, ndev(r), 2)

    def pass_on(slot, member):
        piece = full.at[c, far, member]
        for r in (1, 3, 2):
            send(piece, piece, AGO + slot, fdev(r), 2)
        send(piece, piece, C2 + slot, cdev, 2)
        emit(c, far, member)

    pass_on(0, near)

    landed(GR, gsame.at[0:3])
    landed(GRX, gother)
    total = gmine[...]
    for r in (1, 2, 3):
        total = total + gsame[lax.rem(j + r, N)]
    for p in range(N):
        total = total + gother[p]
    gall[i] = total
    for r in (1, 3, 2):
        send(gall.at[i], gall.at[i], GG, gdev(r), 3)

    for n, r in enumerate((1, 3, 2)):
        landed(AGG + n, mine)
        pass_on(n + 1, lax.rem(near + N - r, N))

    landed(Z2, zs2.at[0 : nz - 1])
    total = zs2[0]
    for r in range(1, nz):
        total = total + zs2[r]
    inverse = lax.rsqrt(gs[i] * (1.0 / hh) + EPS)
    shift = inverse * inverse * inverse * total * (1.0 / hh)
    shift_q = as_column(shift[0:1])
    shift_k = as_column(shift[1:2])
    for index in (DQ, DK, DV):
        landed(index, aqh.at[0:3])
    inverse_k = as_column(inverse[1:2])
    for h in range(N):
        cols = slice(h * HD, (h + 1) * HD)
        dq_buf[:, cols] = (aqh[h].astype(F32) - q_ref[:, cols].astype(F32) * shift_q).astype(BF16)
        grad_k = akh[h].astype(F32) + bkf[h] * inverse_k
        dk_buf[:, cols] = (grad_k - k_ref[:, cols].astype(F32) * shift_k).astype(BF16)
        dv_buf[:, cols] = (avh[h].astype(F32) + bvf[h]).astype(BF16)
    for n, (buf, out) in enumerate(((dq_buf, dq_out), (dk_buf, dk_out), (dv_buf, dv_out))):
        write(buf, out, 1 + n)
    landed(GG, gall.at[0:3])
    for h in range(N):
        gain_buf[0, h] = gall[h, 0:1, :]
        gain_buf[1, h] = gall[h, 1:2, :]
    write(gain_buf, gain_out, 4)

    for slot, back in enumerate((0, 1, 3, 2)):
        landed(AGO + slot, full.at[c, 0:3, 0])
        member = lax.rem(near + N - back, N)
        for r in (1, 3, 2):
            at = full.at[c, lax.rem(far + N - r, N), member]
            send(at, at, C2 + 4 + slot, cdev, 2)
        for r in (1, 3, 2):
            emit(c, lax.rem(far + N - r, N), member)

    for slot, back in enumerate((0, 1, 3, 2)):
        landed(C2 + slot, mine)
        emit(1 - c, near, lax.rem(far + N - back, N))
    for slot, back in enumerate((0, 1, 3, 2)):
        landed(C2 + 4 + slot, full.at[c, 0:3, 0])
        for r in (1, 3, 2):
            emit(1 - c, lax.rem(near + N - r, N), lax.rem(far + N - back, N))

    for group, size in enumerate(sent):
        if group < 3:
            rows = size // (4 * T)
            assert rows * 4 * T == size and rows % 8 == 0
            space = p_all.at[0, 0:rows, :]
        else:
            assert size == tally.shape[0] * 8 * T
            space = tally
        remote(space, space, 0, cdev, group).wait_send()
    for needed, copy in last_parts:
        pl.when(needed)(copy.wait_send)
    pltpu.make_async_copy(kern, kern_out, out_sem.at[0]).wait()
    for copy in written:
        copy.wait()


def finish(
    dq_ref, dk_ref, dv_ref, kern_ref, gain_ref,
    dq_out, dk_out, dv_out, qg_out, kg_out, sk_out, sv_out,
    sems,
):
    pairs = [(kern_ref.at[0, h], sk_out.at[h]) for h in range(N)]
    pairs += [(kern_ref.at[1, h], sv_out.at[h]) for h in range(N)]
    pairs += [(dq_ref, dq_out), (dk_ref, dk_out), (dv_ref, dv_out)]
    pairs += [(gain_ref.at[0], qg_out), (gain_ref.at[1], kg_out)]
    copies = [pltpu.make_async_copy(src, dst, sems.at[n]) for n, (src, dst) in enumerate(pairs)]
    for copy in copies:
        copy.start()
    for copy in copies:
        copy.wait()


def on_device(nz, q, k, v, query_gain, key_gain, key_squeeze, value_squeeze, o):
    width = N * HD
    bf = functools.partial(pltpu.VMEM, dtype=BF16)
    ff = functools.partial(pltpu.VMEM, dtype=F32)
    rows = N * T
    deep = (N + 1) * T
    scratch = [ff((N, 1, HD))] * 2 + [bf((T, width))] * 3
    scratch += [ff((2, N, KS * HD, HD)), ff((2, N, 1, HD))]
    scratch += [bf((T, width))] * 4 + [bf((N, KS * HD, HD))] * 2
    scratch += [bf((rows, HD))] * 4 + [bf((rows, HD))] * 2 + [ff((rows, HD))] * 2
    scratch += [ff((rows, HD)), bf((N * M, KS * HD)), bf((N * M, KS * HD))]
    scratch += [ff((N, 2, T)), ff((nz, N, 2, T)), ff((N, 2, T))]
    scratch += [bf((N, N, M, HD))] * 2 + [bf((N, N * M, HD))] * 2
    scratch += [ff((N, deep, T))] * 2 + [ff((N, N + 1, 1, T)), ff((N, 3, 1, T))]
    scratch += [bf((N, HD, T))] * 2 + [ff((N, HD, T))]
    scratch += [ff((N * M, HD))] * 2 + [bf((N, N, M, HD))] * 4
    scratch += [bf((N, T, HD))] * 3 + [ff((N, 2, T))]
    scratch += [bf((N, T, HD))] * 3 + [ff((N, 2, T)), ff((nz, 2, T))]
    scratch += [bf((N, M, HD))] * 4 + [ff((N, T, HD))] * 2
    scratch += [ff((2, HD))] + [ff((N, 2, HD))] * 3
    scratch += [bf((2, N, HD, HD))] * 2 + [bf((2, N, N, HD, HD))]
    scratch += [ff((18, 2, T))]
    scratch += [
        pltpu.SemaphoreType.DMA((N_SEND,)),
        pltpu.SemaphoreType.DMA((N_RECV,)),
        pltpu.SemaphoreType.DMA((12,)),
        pltpu.SemaphoreType.DMA((5,)),
    ]
    anywhere = pl.BlockSpec(memory_space=pl.ANY)
    hbm = pl.BlockSpec(memory_space=pltpu.MemorySpace.HBM)
    stay = functools.partial(
        pltpu.with_memory_space_constraint, memory_space=pltpu.MemorySpace.HBM
    )
    grads = [jax.ShapeDtypeStruct((T, width), BF16)] * 3
    outs = pl.pallas_call(
        functools.partial(kernel, nz),
        out_shape=grads
        + [
            jax.ShapeDtypeStruct((2, N, KS * HD, HD), F32),
            jax.ShapeDtypeStruct((2, N, 1, HD), F32),
        ],
        in_specs=[hbm] * 8,
        out_specs=[anywhere] * 5,
        scratch_shapes=scratch,
        compiler_params=pltpu.CompilerParams(
            collective_id=0, has_side_effects=True, vmem_limit_bytes=40 * 2**20
        ),
    )(
        stay(q[0]), stay(k[0]), stay(v[0]), stay(o[0]),
        stay(query_gain.reshape(N, 1, HD)), stay(key_gain.reshape(N, 1, HD)),
        stay(key_squeeze), stay(value_squeeze),
    )
    kernels = jax.ShapeDtypeStruct((N, KS * HD, HD), F32)
    gains = jax.ShapeDtypeStruct((N, 1, HD), F32)
    dq, dk, dv, qg, kg, sk, sv = pl.pallas_call(
        finish,
        out_shape=grads + [gains] * 2 + [kernels] * 2,
        in_specs=[anywhere] * 5,
        out_specs=[hbm] * 7,
        scratch_shapes=[pltpu.SemaphoreType.DMA((13,))],
        compiler_params=pltpu.CompilerParams(vmem_limit_bytes=16 * 2**20),
    )(*outs)
    return dq[None], dk[None], dv[None], qg.reshape(width), kg.reshape(width), sk, sv


def solution(mesh):
    by_token = P("dp", "seq", "head")
    by_head = P("head", None, None)
    return jax.shard_map(
        functools.partial(on_device, mesh.shape["head"]),
        mesh=mesh,
        in_specs=(by_token,) * 3 + (P("head"), P("head"), by_head, by_head, by_token),
        out_specs=(by_token,) * 3 + (P("head"), P("head"), by_head, by_head),
        check_vma=False,
    )
```

time: 59.9 us -> 57.1 us (0.953)
  Pallas kernels: 59.1 us -> 56.4 us
    pallas_call x1, Pallas kernels: 56.9 us -> 54.7 us  [on_device(): pl.pallas_call(functools.partial(kernel, nz), out_shape=grads + [jax.Shap...]
where the time goes in v4:
time: 57.1 us; the launch traced here: 57 us
  Pallas kernels  56.4 us (99%)
  between operations  0.64 us (1%)
    pallas_call x1, Pallas kernels, on_device(): pl.pallas_call(functools.partial(kernel, nz), out_shape=grads + [jax.Shap...  54.7 us
    pallas_call x1, Pallas kernels, on_device(): pl.pallas_call(finish, out_shape=grads + [gains] * 2 + [kernels] * 2, in_...  1.68 us

profile of v4, /device:TPU:1, one launch (start us, length us, event | category | flops | bytes accessed | tf_op | source)
XLA Modules:
  0.0 57.0 jit_solution(12987136904265436837)
XLA Ops:
  0.6 54.7 %shard_map.135 = (bf16[256,512]{1,0:T(8,128)(2,1)S(1)}, bf16[256,512]{1,0:T(8,128)(2,1)S(1)}, bf16[256,512]{1,0:T(8,128)(2,1)S(1)}, f32[2,4,512,128]{3,2,1,0:T(8,128)S(1)}, f32[2,4,1,128]{3,2,1,0:T(1,128)S(1)}) custom-call(bf16[256,512]{1,0:T(8,128)(2,1)} %bitcast.11, bf16[256,512]{1,0:T(8,128)(2,1)} %bitcast.12, bf16[256,512]{1,0:T(8,128)(2,1)} %bitcast.13, ...), custom_call_target="tpu_custom_call" | custom-call | tf_op jit(solution)/shard_map/pallas_call | solution.py:590
  55.3 1.7 %shard_map.136 = (bf16[256,512]{1,0:T(8,128)(2,1)}, bf16[256,512]{1,0:T(8,128)(2,1)}, bf16[256,512]{1,0:T(8,128)(2,1)}, f32[4,1,128]{2,1,0:T(1,128)}, f32[4,1,12...) custom-call(bf16[256,512]{1,0:T(8,128)(2,1)S(1)} %get-tuple-element.19.dq_ref, ...), custom_call_target="tpu_custom_call" | custom-call | tf_op jit(solution)/shard_map/pallas_call | solution.py:610

commit v5 on v4

--- a/solution.py
+++ b/solution.py
@@ -71,13 +71,13 @@
     nz,
     q_hbm, k_hbm, v_hbm, o_hbm, gq_hbm, gk_hbm, wk_hbm, wv_hbm,
     dq_out, dk_out, dv_out, kern_out, gain_out,
-    gq_ref, gk_ref, dq_buf, dk_buf, dv_buf, kern, gain_buf, q_ref, k_ref, v_ref, o_ref, wk_ref, wv_ref,
+    gq_ref, gk_ref, q_ref, k_ref, v_ref, o_ref, wk_ref, wv_ref,
     hq, hk, hv, ho, qn, kn, icq, ick, fs, ku, vu, gsp, zs, gs, mkg, mvg, mkc, mvc,
     p_all, g_all, m_all, fin, mkt, knt, dqt, acc_k, acc_v, sbk, sbv, rbk, rbv,
     aq, ak, av, pd, aqh, akh, avh, pdh, zs2,
     gmk, gmv, gmkh, gmvh, bkf, bvf, gmine, gsame, gother, gall,
     pay, rsi, full, tally,
-    ss, rs, loc, out_sem,
+    ss, rs, loc,
 ):
     seq = lax.axis_index("seq")
     x = lax.rem(seq, N)
@@ -135,22 +135,10 @@
     def landed(index, space):
         remote(space, space, index, cdev, 0).wait_recv()
 
-    written = []
-
-    def write(src, dst, index):
-        copy = pltpu.make_async_copy(src, dst, out_sem.at[index])
-        copy.start()
-        written.append(copy)
-
     def emit(core, across, along):
         head = along + core * (across - along)
         rows = pl.ds(pl.multiple_of((across + core * (along - across)) * HD, HD), HD)
-        kern[core, head, rows, :] = full[core, across, along].astype(F32)
-        copy = pltpu.make_async_copy(
-            kern.at[core, head, rows, :], kern_out.at[core, head, rows, :], out_sem.at[0]
-        )
-        copy.start()
-
+        kern_out[core, head, rows, :] = full[core, across, along].astype(F32)
 
     barrier = pltpu.get_barrier_semaphore()
     peers = [gdev(r) for r in (1, 2, 3)] + [odev(r) for r in (1, 2, 3)]
@@ -190,7 +178,7 @@
     own = {}
 
     def exchange(n, src, dst):
-        for r in (1, 3, 2):
+        for r in (2, 1, 3):
             cols = pl.ds(pl.multiple_of(lax.rem(i + r, N) * HD, HD), HD)
             send(src.at[:, cols], dst.at[rows_mine, :], A2A + n, gdev(r), 0)
         cols = pl.ds(pl.multiple_of(i * HD, HD), HD)
@@ -219,7 +207,7 @@
 
     def spread(mem, value, index):
         mem[j] = value.astype(BF16).reshape(N, M, HD)
-        for r in (1, 3, 2):
+        for r in (2, 1, 3):
             send(mem.at[j], mem.at[j], MEM + index, odev(r), 0)
 
     arrived(0)
@@ -254,7 +242,9 @@
     def score(a, block, mask, keys, values):
         at = pl.ds(pl.multiple_of(block * T, T), T)
         rows = slice(a * T, (a + 1) * T)
-        scores = jnp.where(mask, dot_nt(keys, qn[rows, :]), NEG)
+        scores = dot_nt(keys, qn[rows, :])
+        if mask is not None:
+            scores = jnp.where(mask, scores, NEG)
         grads = dot_nt(values, ho[rows, :])
         peak = jnp.max(jnp.max(fold8(scores), 0), 0, keepdims=True)
         lifted = jnp.exp2((scores - peak) * rate)
@@ -287,8 +277,8 @@
 
         def absorb(b, current, a=a):
             old_peak, old_mass, old_weighted = current
-            limit = jnp.where(b == a, j * M, T)
-            peak, mass, weighted = score(a, b + 1, key_at < limit, mkc[b], mvc[b])
+            mask = None if isinstance(b, int) else key_at < j * M
+            peak, mass, weighted = score(a, b + 1, mask, mkc[b], mvc[b])
             top = jnp.maximum(old_peak, peak)
             old_factor = jnp.exp2((old_peak - top) * rate)
             factor = jnp.exp2((peak - top) * rate)
@@ -298,7 +288,10 @@
                 old_weighted * old_factor + weighted * factor,
             )
 
-        peak, mass, weighted = lax.fori_loop(0, a + 1 - past, absorb, state[a])
+        current = state[a]
+        for b in range(a):
+            current = absorb(b, current)
+        peak, mass, weighted = lax.fori_loop(a + past, a + 1, absorb, current)
         inverse_mass = 1.0 / mass
         fin[a, 0] = peak
         fin[a, 1] = inverse_mass
@@ -322,32 +315,30 @@
         total = jnp.sum(fold8(grad * raw_full * inv), 0)
         return total, (gained * inv).astype(BF16), row_sum(gained * raw_full)
 
-    gain_k_sum = jnp.zeros((8, HD), F32)
-    for a in range(N):
-        rows = slice(a * T, (a + 1) * T)
-        attend, d_scores = settle(a, 0)
-        dqt[a] = dot_nn(knt[a], d_scores)
-        grad_k = dot_nn(d_scores, qn[rows, :]) * scale
-        av[a] = dot_nn(attend, ho[rows, :]).astype(BF16)
-        total, ak[a], pd[a, 1:2, :] = norm_side(grad_k, hk[rows, :], ick[rows, :], gain_k)
-        gain_k_sum = gain_k_sum + total
-    homeward(av, avh, DV)
-    homeward(ak, akh, DK)
-
     last_parts = []
     for b in range(N):
-        acc_k[...] = jnp.zeros((T, HD), F32)
-        acc_v[...] = jnp.zeros((T, HD), F32)
-
-        def add_up(a, nothing, b=b):
-            rows = pl.ds(pl.multiple_of(a * T, T), T)
-            attend, d_scores = settle(a, b + 1)
+        after = range(b + 1, N)
+        settled = [settle(a, b + 1) for a in after]
+        for a, (_, d_scores) in zip(after, settled):
+            part = dot_nn(mkt[b], d_scores)
+            dqt[a] = part if b == 0 else dqt[a] + part
+        if settled:
+            rows = slice((b + 1) * T, N * T)
+            acc_k[...] = dot_nn(jnp.concatenate([d for _, d in settled], 1), qn[rows, :])
+            acc_v[...] = dot_nn(jnp.concatenate([p for p, _ in settled], 1), ho[rows, :])
+        else:
+            acc_k[...] = jnp.zeros((T, HD), F32)
+            acc_v[...] = jnp.zeros((T, HD), F32)
+        if b == 0:
+            dqt[0] = jnp.zeros((HD, T), F32)
+
+        @pl.when(j > 0)
+        def _(b=b):
+            rows = slice(b * T, (b + 1) * T)
+            attend, d_scores = settle(b, b + 1)
             acc_k[...] = acc_k[...] + dot_nn(d_scores, qn[rows, :])
             acc_v[...] = acc_v[...] + dot_nn(attend, ho[rows, :])
-            dqt[a] = dqt[a] + dot_nn(mkt[b], d_scores)
-            return nothing
-
-        lax.fori_loop(b + past, N, add_up, 0)
+            dqt[b] = dqt[b] + dot_nn(mkt[b], d_scores)
 
         sbk[b] = (acc_k[...] * scale).astype(BF16).reshape(N, M, HD)
         sbv[b] = acc_v[...].astype(BF16).reshape(N, M, HD)
@@ -362,6 +353,18 @@
                     pl.when(to < j)(copy.start)
                     last_parts.append((to < j, copy))
 
+    gain_k_sum = jnp.zeros((8, HD), F32)
+    for a in range(N):
+        rows = slice(a * T, (a + 1) * T)
+        attend, d_scores = settle(a, 0)
+        dqt[a] = dqt[a] + dot_nn(knt[a], d_scores)
+        grad_k = dot_nn(d_scores, qn[rows, :]) * scale
+        av[a] = dot_nn(attend, ho[rows, :]).astype(BF16)
+        total, ak[a], pd[a, 1:2, :] = norm_side(grad_k, hk[rows, :], ick[rows, :], gain_k)
+        gain_k_sum = gain_k_sum + total
+    homeward(av, avh, DV)
+    homeward(ak, akh, DK)
+
     gain_q_sum = jnp.zeros((8, HD), F32)
     for a in range(N):
         rows = slice(a * T, (a + 1) * T)
@@ -401,10 +404,11 @@
     gmk[...] = grad_mem_k.reshape(N, M, HD)
     gmv[...] = grad_mem_v.reshape(N, M, HD)
 
-    for p in range(N):
-        send(pay.at[1 - c, p], rsi.at[1, j], RSX, cross(p), 2)
-    for r in (1, 3, 2):
-        send(pay.at[c, lax.rem(j + r, N)], rsi.at[0, j], RS, odev(r), 2)
+    for r in (2, 1, 3):
+        to = lax.rem(j + r, N)
+        send(pay.at[1 - c, to], rsi.at[1, j], RSX, cross(to), 2)
+        send(pay.at[c, to], rsi.at[0, j], RS, odev(r), 2)
+    send(pay.at[1 - c, j], rsi.at[1, j], RSX, cross(j), 2)
     homeward(gmk, gmkh, GM)
     homeward(gmv, gmvh, GM + 1)
 
@@ -418,6 +422,38 @@
         send(gmine, gsame.at[j], GR, odev(r), 3)
     for p in range(N):
         send(gmine, gother.at[j], GRX, cross(p), 3)
+
+    landed(RSX, rsi.at[1])
+    landed(RS, rsi.at[0, 0:3])
+    total = pay[c, j].astype(F32)
+    for r in (1, 2, 3):
+        total = total + rsi[0, lax.rem(j + r, N)].astype(F32)
+    for p in range(N):
+        total = total + rsi[1, p].astype(F32)
+    full[c, far, near] = total.astype(BF16)
+    mine = full.at[c, far, near]
+    for n, r in enumerate((1, 3, 2)):
+        send(mine, mine, AGG + n, ndev(r), 2)
+
+    def pass_on(slot, member):
+        piece = full.at[c, far, member]
+        for r in (2, 1, 3):
+            send(piece, piece, AGO + slot, fdev(r), 2)
+        send(piece, piece, C2 + slot, cdev, 2)
+        emit(c, far, member)
+
+    pass_on(0, near)
+
+    landed(GR, gsame.at[0:3])
+    landed(GRX, gother)
+    total = gmine[...]
+    for r in (1, 2, 3):
+        total = total + gsame[lax.rem(j + r, N)]
+    for p in range(N):
+        total = total + gother[p]
+    gall[i] = total
+    for r in (1, 3, 2):
+        send(gall.at[i], gall.at[i], GG, gdev(r), 3)
 
     landed(GM, gmkh.at[0:3])
     landed(GM + 1, gmvh.at[0:3])
@@ -443,41 +479,20 @@
     for r in range(1, nz):
         send(zs2.at[z], zs2.at[z], Z2, zdev(r), 3)
 
-    landed(RSX, rsi.at[1])
-    landed(RS, rsi.at[0, 0:3])
-    total = pay[c, j].astype(F32)
-    for r in (1, 2, 3):
-        total = total + rsi[0, lax.rem(j + r, N)].astype(F32)
-    for p in range(N):
-        total = total + rsi[1, p].astype(F32)
-    full[c, far, near] = total.astype(BF16)
-    mine = full.at[c, far, near]
-    for n, r in enumerate((1, 3, 2)):
-        send(mine, mine, AGG + n, ndev(r), 2)
-
-    def pass_on(slot, member):
-        piece = full.at[c, far, member]
-        for r in (1, 3, 2):
-            send(piece, piece, AGO + slot, fdev(r), 2)
-        send(piece, piece, C2 + slot, cdev, 2)
-        emit(c, far, member)
-
-    pass_on(0, near)
-
-    landed(GR, gsame.at[0:3])
-    landed(GRX, gother)
-    total = gmine[...]
-    for r in (1, 2, 3):
-        total = total + gsame[lax.rem(j + r, N)]
-    for p in range(N):
-        total = total + gother[p]
-    gall[i] = total
-    for r in (1, 3, 2):
-        send(gall.at[i], gall.at[i], GG, gdev(r), 3)
-
     for n, r in enumerate((1, 3, 2)):
         landed(AGG + n, mine)
         pass_on(n + 1, lax.rem(near + N - r, N))
+
+    for slot, back in enumerate((0, 1, 3, 2)):
+        landed(AGO + slot, full.at[c, 0:3, 0])
+        member = lax.rem(near + N - back, N)
+        for r in (1, 3, 2):
+            at = full.at[c, lax.rem(far + N - r, N), member]
+            send(at, at, C2 + 4 + slot, cdev, 2)
+        for r in (1, 3, 2):
+            emit(c, lax.rem(far + N - r, N), member)
+        landed(C2 + slot, mine)
+        emit(1 - c, near, lax.rem(far + N - back, N))
 
     landed(Z2, zs2.at[0 : nz - 1])
     total = zs2[0]
@@ -492,30 +507,15 @@
     inverse_k = as_column(inverse[1:2])
     for h in range(N):
         cols = slice(h * HD, (h + 1) * HD)
-        dq_buf[:, cols] = (aqh[h].astype(F32) - q_ref[:, cols].astype(F32) * shift_q).astype(BF16)
+        dq_out[:, cols] = (aqh[h].astype(F32) - q_ref[:, cols].astype(F32) * shift_q).astype(BF16)
         grad_k = akh[h].astype(F32) + bkf[h] * inverse_k
-        dk_buf[:, cols] = (grad_k - k_ref[:, cols].astype(F32) * shift_k).astype(BF16)
-        dv_buf[:, cols] = (avh[h].astype(F32) + bvf[h]).astype(BF16)
-    for n, (buf, out) in enumerate(((dq_buf, dq_out), (dk_buf, dk_out), (dv_buf, dv_out))):
-        write(buf, out, 1 + n)
+        dk_out[:, cols] = (grad_k - k_ref[:, cols].astype(F32) * shift_k).astype(BF16)
+        dv_out[:, cols] = (avh[h].astype(F32) + bvf[h]).astype(BF16)
     landed(GG, gall.at[0:3])
     for h in range(N):
-        gain_buf[0, h] = gall[h, 0:1, :]
-        gain_buf[1, h] = gall[h, 1:2, :]
-    write(gain_buf, gain_out, 4)
-
-    for slot, back in enumerate((0, 1, 3, 2)):
-        landed(AGO + slot, full.at[c, 0:3, 0])
-        member = lax.rem(near + N - back, N)
-        for r in (1, 3, 2):
-            at = full.at[c, lax.rem(far + N - r, N), member]
-            send(at, at, C2 + 4 + slot, cdev, 2)
-        for r in (1, 3, 2):
-            emit(c, lax.rem(far + N - r, N), member)
-
-    for slot, back in enumerate((0, 1, 3, 2)):
-        landed(C2 + slot, mine)
-        emit(1 - c, near, lax.rem(far + N - back, N))
+        gain_out[0, h] = gall[h, 0:1, :]
+        gain_out[1, h] = gall[h, 1:2, :]
+
     for slot, back in enumerate((0, 1, 3, 2)):
         landed(C2 + 4 + slot, full.at[c, 0:3, 0])
         for r in (1, 3, 2):
@@ -532,9 +532,6 @@
         remote(space, space, 0, cdev, group).wait_send()
     for needed, copy in last_parts:
         pl.when(needed)(copy.wait_send)
-    pltpu.make_async_copy(kern, kern_out, out_sem.at[0]).wait()
-    for copy in written:
-        copy.wait()
 
 
 def finish(
@@ -559,8 +556,7 @@
     ff = functools.partial(pltpu.VMEM, dtype=F32)
     rows = N * T
     deep = (N + 1) * T
-    scratch = [ff((N, 1, HD))] * 2 + [bf((T, width))] * 3
-    scratch += [ff((2, N, KS * HD, HD)), ff((2, N, 1, HD))]
+    scratch = [ff((N, 1, HD))] * 2
     scratch += [bf((T, width))] * 4 + [bf((N, KS * HD, HD))] * 2
     scratch += [bf((rows, HD))] * 4 + [bf((rows, HD))] * 2 + [ff((rows, HD))] * 2
     scratch += [ff((rows, HD)), bf((N * M, KS * HD)), bf((N * M, KS * HD))]
@@ -579,8 +575,8 @@
         pltpu.SemaphoreType.DMA((N_SEND,)),
         pltpu.SemaphoreType.DMA((N_RECV,)),
         pltpu.SemaphoreType.DMA((12,)),
-        pltpu.SemaphoreType.DMA((5,)),
     ]
+    vmem = pl.BlockSpec(memory_space=pltpu.VMEM)
     anywhere = pl.BlockSpec(memory_space=pl.ANY)
     hbm = pl.BlockSpec(memory_space=pltpu.MemorySpace.HBM)
     stay = functools.partial(
@@ -595,7 +591,7 @@
             jax.ShapeDtypeStruct((2, N, 1, HD), F32),
         ],
         in_specs=[hbm] * 8,
-        out_specs=[anywhere] * 5,
+        out_specs=[vmem] * 5,
         scratch_shapes=scratch,
         compiler_params=pltpu.CompilerParams(
             collective_id=0, has_side_effects=True, vmem_limit_bytes=40 * 2**20

time: 57.1 us -> 52.9 us (0.926)
  Pallas kernels: 56.4 us -> 52.2 us
    pallas_call x1, Pallas kernels: 54.7 us -> 50.5 us  [on_device(): pl.pallas_call(functools.partial(kernel, nz), out_shape=grads + [jax.Shap...]
where the time goes in v5:
time: 52.9 us; the launch traced here: 52.8 us
  Pallas kernels  52.2 us (99%)
  between operations  0.64 us (1%)
    pallas_call x1, Pallas kernels, on_device(): pl.pallas_call(functools.partial(kernel, nz), out_shape=grads + [jax.Shap...  50.5 us
    pallas_call x1, Pallas kernels, on_device(): pl.pallas_call(finish, out_shape=grads + [gains] * 2 + [kernels] * 2, in_...  1.68 us

profile of v5, /device:TPU:1, one launch (start us, length us, event | category | flops | bytes accessed | tf_op | source)
XLA Modules:
  0.0 52.8 jit_solution(5532749776450649059)
XLA Ops:
  0.6 50.5 %shard_map.135 = (bf16[256,512]{1,0:T(8,128)(2,1)S(1)}, bf16[256,512]{1,0:T(8,128)(2,1)S(1)}, bf16[256,512]{1,0:T(8,128)(2,1)S(1)}, f32[2,4,512,128]{3,2,1,0:T(8,128)S(1)}, f32[2,4,1,128]{3,2,1,0:T(1,128)S(1)}) custom-call(bf16[256,512]{1,0:T(8,128)(2,1)} %bitcast.11, bf16[256,512]{1,0:T(8,128)(2,1)} %bitcast.12, bf16[256,512]{1,0:T(8,128)(2,1)} %bitcast.13, ...), custom_call_target="tpu_custom_call" | custom-call | tf_op jit(solution)/shard_map/pallas_call | solution.py:586
  51.1 1.7 %shard_map.136 = (bf16[256,512]{1,0:T(8,128)(2,1)}, bf16[256,512]{1,0:T(8,128)(2,1)}, bf16[256,512]{1,0:T(8,128)(2,1)}, f32[4,1,128]{2,1,0:T(1,128)}, f32[4,1,12...) custom-call(bf16[256,512]{1,0:T(8,128)(2,1)S(1)} %get-tuple-element.19.dq_ref, ...), custom_call_target="tpu_custom_call" | custom-call | tf_op jit(solution)/shard_map/pallas_call | solution.py:606

commit v6 on v5

--- a/solution.py
+++ b/solution.py
@@ -316,12 +316,14 @@
         return total, (gained * inv).astype(BF16), row_sum(gained * raw_full)
 
     last_parts = []
-    for b in range(N):
+    for a in range(N):
+        dqt[a] = jnp.zeros((HD, T), F32)
+    for b in range(N - 1, -1, -1):
         after = range(b + 1, N)
         settled = [settle(a, b + 1) for a in after]
         for a, (_, d_scores) in zip(after, settled):
             part = dot_nn(mkt[b], d_scores)
-            dqt[a] = part if b == 0 else dqt[a] + part
+            dqt[a] = dqt[a] + part
         if settled:
             rows = slice((b + 1) * T, N * T)
             acc_k[...] = dot_nn(jnp.concatenate([d for _, d in settled], 1), qn[rows, :])
@@ -329,8 +331,6 @@
         else:
             acc_k[...] = jnp.zeros((T, HD), F32)
             acc_v[...] = jnp.zeros((T, HD), F32)
-        if b == 0:
-            dqt[0] = jnp.zeros((HD, T), F32)
 
         @pl.when(j > 0)
         def _(b=b):
@@ -454,6 +454,13 @@
     gall[i] = total
     for r in (1, 3, 2):
         send(gall.at[i], gall.at[i], GG, gdev(r), 3)
+
+    def forward(n, r):
+        landed(AGG + n, mine)
+        pass_on(n + 1, lax.rem(near + N - r, N))
+
+    forward(0, 1)
+    forward(1, 3)
 
     landed(GM, gmkh.at[0:3])
     landed(GM + 1, gmvh.at[0:3])
@@ -479,9 +486,7 @@
     for r in range(1, nz):
         send(zs2.at[z], zs2.at[z], Z2, zdev(r), 3)
 
-    for n, r in enumerate((1, 3, 2)):
-        landed(AGG + n, mine)
-        pass_on(n + 1, lax.rem(near + N - r, N))
+    forward(2, 2)
 
     for slot, back in enumerate((0, 1, 3, 2)):
         landed(AGO + slot, full.at[c, 0:3, 0])

time: 52.9 us -> 52.1 us (0.985)
  Pallas kernels: 52.2 us -> 51.4 us
    pallas_call x1, Pallas kernels: 50.5 us -> 49.7 us  [on_device(): pl.pallas_call(functools.partial(kernel, nz), out_shape=grads + [jax.Shap...]
where the time goes in v6:
time: 52.1 us; the launch traced here: 52 us
  Pallas kernels  51.4 us (99%)
  between operations  0.64 us (1%)
    pallas_call x1, Pallas kernels, on_device(): pl.pallas_call(functools.partial(kernel, nz), out_shape=grads + [jax.Shap...  49.7 us
    pallas_call x1, Pallas kernels, on_device(): pl.pallas_call(finish, out_shape=grads + [gains] * 2 + [kernels] * 2, in_...  1.68 us

profile of v6, /device:TPU:1, one launch (start us, length us, event | category | flops | bytes accessed | tf_op | source)
XLA Modules:
  0.0 52.0 jit_solution(1324291441125038665)
XLA Ops:
  0.6 49.7 %shard_map.135 = (bf16[256,512]{1,0:T(8,128)(2,1)S(1)}, bf16[256,512]{1,0:T(8,128)(2,1)S(1)}, bf16[256,512]{1,0:T(8,128)(2,1)S(1)}, f32[2,4,512,128]{3,2,1,0:T(8,128)S(1)}, f32[2,4,1,128]{3,2,1,0:T(1,128)S(1)}) custom-call(bf16[256,512]{1,0:T(8,128)(2,1)} %bitcast.11, bf16[256,512]{1,0:T(8,128)(2,1)} %bitcast.12, bf16[256,512]{1,0:T(8,128)(2,1)} %bitcast.13, ...), custom_call_target="tpu_custom_call" | custom-call | tf_op jit(solution)/shard_map/pallas_call | solution.py:591
  50.3 1.7 %shard_map.136 = (bf16[256,512]{1,0:T(8,128)(2,1)}, bf16[256,512]{1,0:T(8,128)(2,1)}, bf16[256,512]{1,0:T(8,128)(2,1)}, f32[4,1,128]{2,1,0:T(1,128)}, f32[4,1,12...) custom-call(bf16[256,512]{1,0:T(8,128)(2,1)S(1)} %get-tuple-element.19.dq_ref, ...), custom_call_target="tpu_custom_call" | custom-call | tf_op jit(solution)/shard_map/pallas_call | solution.py:611

commit v7 on v6

--- a/solution.py
+++ b/solution.py
@@ -196,7 +196,7 @@
     exchange(3, o_ref, ho)
 
     landed(G1, gsp.at[0:3])
-    for r in range(1, nz):
+    for r in sorted(range(1, nz), key=lambda r: -min(r, nz - r)):
         send(gsp, zs.at[z], Z1, zdev(r), 0)
     for copy in loads[4:]:
         copy.wait()
@@ -306,7 +306,7 @@
 
     def homeward(src, dst, index, group=1):
         dst[i] = src[i]
-        for r in (1, 3, 2):
+        for r in (2, 1, 3):
             send(src.at[lax.rem(i + r, N)], dst.at[i], index, gdev(r), group)
 
     def norm_side(grad, raw, inv, gain):
@@ -432,7 +432,7 @@
         total = total + rsi[1, p].astype(F32)
     full[c, far, near] = total.astype(BF16)
     mine = full.at[c, far, near]
-    for n, r in enumerate((1, 3, 2)):
+    for n, r in ((2, 2), (0, 1), (1, 3)):
         send(mine, mine, AGG + n, ndev(r), 2)
 
     def pass_on(slot, member):
@@ -483,7 +483,7 @@
         total = total + pdh[h]
     zs2[z, 0:1, :] = total[0:1]
     zs2[z, 1:2, :] = total[1:2] + row_sum(product)
-    for r in range(1, nz):
+    for r in sorted(range(1, nz), key=lambda r: -min(r, nz - r)):
         send(zs2.at[z], zs2.at[z], Z2, zdev(r), 3)
 
     forward(2, 2)

time: 52.1 us -> 52 us (level)
  no operation moved by 1% of the time
where the time goes in v7:
time: 52 us; the launch traced here: 51.9 us
  Pallas kernels  51.2 us (98%)
  between operations  0.64 us (1%)
    pallas_call x1, Pallas kernels, on_device(): pl.pallas_call(functools.partial(kernel, nz), out_shape=grads + [jax.Shap...  49.5 us
    pallas_call x1, Pallas kernels, on_device(): pl.pallas_call(finish, out_shape=grads + [gains] * 2 + [kernels] * 2, in_...  1.68 us

profile of v7, /device:TPU:1, one launch (start us, length us, event | category | flops | bytes accessed | tf_op | source)
XLA Modules:
  0.0 51.9 jit_solution(8807156465842491054)
XLA Ops:
  0.6 49.5 %shard_map.135 = (bf16[256,512]{1,0:T(8,128)(2,1)S(1)}, bf16[256,512]{1,0:T(8,128)(2,1)S(1)}, bf16[256,512]{1,0:T(8,128)(2,1)S(1)}, f32[2,4,512,128]{3,2,1,0:T(8,128)S(1)}, f32[2,4,1,128]{3,2,1,0:T(1,128)S(1)}) custom-call(bf16[256,512]{1,0:T(8,128)(2,1)} %bitcast.11, bf16[256,512]{1,0:T(8,128)(2,1)} %bitcast.12, bf16[256,512]{1,0:T(8,128)(2,1)} %bitcast.13, ...), custom_call_target="tpu_custom_call" | custom-call | tf_op jit(solution)/shard_map/pallas_call | solution.py:591
  50.2 1.7 %shard_map.136 = (bf16[256,512]{1,0:T(8,128)(2,1)}, bf16[256,512]{1,0:T(8,128)(2,1)}, bf16[256,512]{1,0:T(8,128)(2,1)}, f32[4,1,128]{2,1,0:T(1,128)}, f32[4,1,12...) custom-call(bf16[256,512]{1,0:T(8,128)(2,1)S(1)} %get-tuple-element.19.dq_ref, ...), custom_call_target="tpu_custom_call" | custom-call | tf_op jit(solution)/shard_map/pallas_call | solution.py:611

commit v8 on v7

--- a/solution.py
+++ b/solution.py
@@ -142,7 +142,7 @@
 
     barrier = pltpu.get_barrier_semaphore()
     peers = [gdev(r) for r in (1, 2, 3)] + [odev(r) for r in (1, 2, 3)]
-    peers += [zdev(r) for r in range(1, nz)] + [cross(p) for p in range(N)] + [cdev]
+    peers += [zdev(r) for r in range(1, nz)] + [cross(p) for p in range(N)]
     for peer in peers:
         pl.semaphore_signal(barrier, inc=1, device_id=peer, device_id_type=MESH)
 
@@ -224,16 +224,22 @@
     arrived(1)
     for a in range(N):
         rows = slice(a * T, (a + 1) * T)
-        inverse = lax.rsqrt(gs[a] * (1.0 / hh) + EPS)
-        icq[rows, :] = as_column(inverse[0:1])
-        ick[rows, :] = as_column(inverse[1:2])
+        ick[rows, :] = as_column(lax.rsqrt(gs[a, 1:2, :] * (1.0 / hh) + EPS))
         normed = (hk[rows, :].astype(F32) * ick[rows, :] * gain_k).astype(BF16)
         kn[rows, :] = normed
         fs[rows, :] = normed.astype(F32)
     unfold(ku)
     spread(mkg, dot_nn(ku[...], wk_ref[i]), 0)
 
+    for a in range(N):
+        rows = slice(a * T, (a + 1) * T)
+        icq[rows, :] = as_column(lax.rsqrt(gs[a, 0:1, :] * (1.0 / hh) + EPS))
+        knt[a] = jnp.transpose(kn[rows, :])
+
     arrived(2)
+    for a in range(N):
+        rows = slice(a * T, (a + 1) * T)
+        qn[rows, :] = (hq[rows, :].astype(F32) * icq[rows, :] * gain_q).astype(BF16)
     arrived(3)
     key_at = lax.broadcasted_iota(jnp.int32, (T, T), 0)
     query_at = lax.broadcasted_iota(jnp.int32, (T, T), 1)
@@ -258,9 +264,7 @@
     state = []
     for a in range(N):
         rows = slice(a * T, (a + 1) * T)
-        qn[rows, :] = (hq[rows, :].astype(F32) * icq[rows, :] * gain_q).astype(BF16)
         state.append(score(a, 0, key_at <= query_at, kn[rows, :], hv[rows, :]))
-        knt[a] = jnp.transpose(kn[rows, :])
 
     landed(MEM, mkg.at[0:3])
     landed(MEM + 1, mvg.at[0:3])

time: 52 us -> 51.9 us (level)
  no operation moved by 1% of the time
where the time goes in v8:
time: 51.9 us; the launch traced here: 51.8 us
  Pallas kernels  51.2 us (99%)
  between operations  0.64 us (1%)
    pallas_call x1, Pallas kernels, on_device(): pl.pallas_call(functools.partial(kernel, nz), out_shape=grads + [jax.Shap...  49.5 us
    pallas_call x1, Pallas kernels, on_device(): pl.pallas_call(finish, out_shape=grads + [gains] * 2 + [kernels] * 2, in_...  1.68 us

profile of v8, /device:TPU:1, one launch (start us, length us, event | category | flops | bytes accessed | tf_op | source)
XLA Modules:
  0.0 51.8 jit_solution(17232357583281150272)
XLA Ops:
  0.6 49.5 %shard_map.135 = (bf16[256,512]{1,0:T(8,128)(2,1)S(1)}, bf16[256,512]{1,0:T(8,128)(2,1)S(1)}, bf16[256,512]{1,0:T(8,128)(2,1)S(1)}, f32[2,4,512,128]{3,2,1,0:T(8,128)S(1)}, f32[2,4,1,128]{3,2,1,0:T(1,128)S(1)}) custom-call(bf16[256,512]{1,0:T(8,128)(2,1)} %bitcast.11, bf16[256,512]{1,0:T(8,128)(2,1)} %bitcast.12, bf16[256,512]{1,0:T(8,128)(2,1)} %bitcast.13, ...), custom_call_target="tpu_custom_call" | custom-call | tf_op jit(solution)/shard_map/pallas_call | solution.py:595
  50.1 1.7 %shard_map.136 = (bf16[256,512]{1,0:T(8,128)(2,1)}, bf16[256,512]{1,0:T(8,128)(2,1)}, bf16[256,512]{1,0:T(8,128)(2,1)}, f32[4,1,128]{2,1,0:T(1,128)}, f32[4,1,12...) custom-call(bf16[256,512]{1,0:T(8,128)(2,1)S(1)} %get-tuple-element.19.dq_ref, ...), custom_call_target="tpu_custom_call" | custom-call | tf_op jit(solution)/shard_map/pallas_call | solution.py:615
